TPU v7x, 128 devices: a whole 4x4x4 slice. The times are simulated.
128 devices in a mesh: grp: 8 (over x_hi, y), blk: 16 (over z, x_lo, core).
Axes of the slice: x: 4 (x_hi: 2, x_lo: 2; x = x_hi * 2 + x_lo), y: 4, z: 4, core: 2. Of those that a mesh axis runs over, the one named last changes fastest.
Arguments:
- queries: bfloat16 [8, 2048, 4096], P('grp', 'blk'), may hold values from -5 to 5
- keys: bfloat16 [8, 2048, 256], P('grp', 'blk'), may hold values from -5 to 5
- values: bfloat16 [8, 2048, 256], P('grp', 'blk'), may hold values from -6 to 6
- stream: bfloat16 [8, 2048, 4096], P('grp', 'blk'), may hold values from -6 to 6
- norm_gain: float32 [4096], replicated, may hold values from 0.1 to 1.9
- router_weight: bfloat16 [4096, 128], replicated, may hold values from -0.09375 to 0.09375
- gate_weight: bfloat16 [128, 4096, 768], P(('grp', 'blk')), may hold values from -0.09375 to 0.09375
- up_weight: bfloat16 [128, 4096, 768], P(('grp', 'blk')), may hold values from -0.09375 to 0.09375
- down_weight: bfloat16 [128, 768, 4096], P(('grp', 'blk')), may hold values from -0.21875 to 0.21875
- doc_lengths: int32 [8, 4], P('grp'), may hold values from 1 to 1536, 2048 in all within a row
- expert_ids: int32 [8, 2048, 2], P('grp', 'blk'), may hold values from 0 to 127, all different within a row; in each aligned block of 128 rows (0 to 127, 128 to 255, ..., all dimensions but the last counted through in order) at most 3 rows name the same one
- out_grad: bfloat16 [8, 2048, 4096], P('grp', 'blk'), may hold values from -6 to 6
Outputs:
- query_grad: bfloat16 [8, 2048, 4096], P('grp', 'blk')
- key_gradient_rows: bfloat16 [8, 2048, 256], P('grp', 'blk')
- value_gradient_rows: bfloat16 [8, 2048, 256], P('grp', 'blk')
- residual_gradient: bfloat16 [8, 2048, 4096], P('grp', 'blk')
- router_grad: float32 [4096, 128], P(('grp', 'blk'))
Inputs may be any that keep to these rules, and one draw needn't show every extreme that they name: `doc_lengths`: each row sums to 2048; the longest document of every sequence holds exactly (6144) // 4 tokens. `expert_ids`: each token names 2 different experts. Among the 128 tokens of one device no expert is named more than 3 times, and in some devices one expert is named exactly 3 times.
All inputs are finite; a program needn't handle non-finite values.
Results may differ from a plain program's by a relative error of at most 0.035.
Values may be sent and summed in bfloat16 or wider, within the bound.
No kernel may reach another device: no remote copies, remote signals or barrier semaphores. Data moves between devices by JAX's collectives and lax.ppermute only.
A program may use at most 128 MiB of HBM per device.

v0:
```python
import math

import jax
import jax.numpy as jnp
from jax import lax
from jax.experimental import pallas as pl
from jax.experimental.pallas import tpu as pltpu
from jax.sharding import Mesh
from jax.sharding import PartitionSpec as P


HEAD_SIZE = 128
QUERY_HEADS = 32
KEY_VALUE_HEADS = 2
HEADS_PER_GROUP = QUERY_HEADS // KEY_VALUE_HEADS
BLK = ("blk_0", "blk_1", "blk_2")
GRP_BLK = ("grp_0", "grp_1", "blk_0", "blk_1", "blk_2")
GRP = ("grp_0", "grp_1")
ZX = ("blk_0", "blk_1")
CORE = "blk_2"

NEGATIVE_HUGE = -1e30
EPSILON = 1e-06
SCALE = HEAD_SIZE ** (-0.5)
KEY_BLOCK = 256
OCTET = 8
VMEM_LIMIT = 60 * 1024 * 1024
PITCH = QUERY_HEADS + 1

NT = (((1,), (1,)), ((), ()))
TN = (((0,), (0,)), ((), ()))


def dot32(a, b, dims=(((1,), (0,)), ((), ()))):
    return lax.dot_general(a, b, dims, preferred_element_type=jnp.float32)


def lanes(start, size):
    return pl.ds(pl.multiple_of(start, 128), size)


def order_blocks(mine_ref, theirs_ref, core, kv_scr):
    is_first = jnp.full((128, mine_ref.shape[2]), core, jnp.int32) == 0

    def place(b, _):
        mine = mine_ref[b].astype(jnp.float32)
        theirs = theirs_ref[b].astype(jnp.float32)
        start = pl.multiple_of(b * KEY_BLOCK, KEY_BLOCK)
        kv_scr[pl.ds(start, 128), :] = jnp.where(is_first, mine, theirs).astype(jnp.bfloat16)
        kv_scr[pl.ds(start + 128, 128), :] = jnp.where(is_first, theirs, mine).astype(jnp.bfloat16)
        return 0

    lax.fori_loop(0, mine_ref.shape[0], place, 0)


def attend_kernel(
    meta,
    slots,
    q_ref,
    mine_ref,
    theirs_ref,
    stream_ref,
    gain_ref,
    w_ref,
    linv_ref,
    att_ref,
    hid_ref,
    norm_ref,
    rms_ref,
    send_ref,
    kv_scr,
    vt_scr,
    bias_scr,
    s_scr,
    ot_scr,
    ss_scr,
    rows_scr,
):
    octet = pl.program_id(0)
    group = octet // (HEADS_PER_GROUP // OCTET)
    low, high, core, first_query = meta[0], meta[1], meta[2], meta[3]
    tokens = q_ref.shape[0]
    factor = SCALE * math.log2(math.e)

    @pl.when(octet == 0)
    def _():
        order_blocks(mine_ref, theirs_ref, core, kv_scr)
        ss_scr[...] = jnp.zeros_like(ss_scr)
        query = first_query + lax.broadcasted_iota(jnp.int32, (KEY_BLOCK, tokens), 1)
        start = jnp.zeros((KEY_BLOCK, tokens), jnp.int32)
        for d in range(4):
            start = jnp.maximum(start, jnp.where(query >= meta[4 + d], meta[4 + d], 0))

        def prepare(kb, _):
            rows = pl.ds(pl.multiple_of(kb * KEY_BLOCK, KEY_BLOCK), KEY_BLOCK)
            vt_scr[kb] = kv_scr[rows, 256:512].T
            key = kb * KEY_BLOCK + lax.broadcasted_iota(jnp.int32, (KEY_BLOCK, tokens), 0)
            seen = (key <= query) & (key >= start)
            bias_scr[kb] = jnp.where(seen, 0.0, NEGATIVE_HUGE)
            return 0

        lax.fori_loop(low, high + 1, prepare, 0)

    pairs = OCTET // 2
    wide = 2 * tokens

    def score(kb, tops):
        rows = pl.ds(pl.multiple_of(kb * KEY_BLOCK, KEY_BLOCK), KEY_BLOCK)
        key_rows = kv_scr[rows, lanes(group * HEAD_SIZE, HEAD_SIZE)]
        bias = bias_scr[kb]
        bias = jnp.concatenate([bias, bias], axis=1)
        new = []
        for p in range(pairs):
            c = 2 * p * HEAD_SIZE
            both = jnp.concatenate(
                [q_ref[:, c : c + HEAD_SIZE], q_ref[:, c + HEAD_SIZE : c + 2 * HEAD_SIZE]], axis=0
            )
            s = dot32(key_rows, both, NT) + bias
            s_scr[kb, :, p * wide : (p + 1) * wide] = s
            new.append(jnp.maximum(tops[p], jnp.max(s.reshape(-1, 8, wide), axis=0)))
        return tuple(new)

    tops = lax.fori_loop(
        low, high + 1, score, tuple(jnp.full((8, wide), NEGATIVE_HUGE, jnp.float32) for _ in range(pairs))
    )
    tops = tuple(jnp.max(t, axis=0, keepdims=True) * factor for t in tops)
    ot_scr[...] = jnp.zeros_like(ot_scr)

    def weigh(kb, sums):
        value_cols = vt_scr[kb, pl.ds(pl.multiple_of(group * HEAD_SIZE, HEAD_SIZE), HEAD_SIZE), :]
        new = []
        for p in range(pairs):
            span = slice(p * wide, (p + 1) * wide)
            w = jnp.exp2(s_scr[kb, :, span] * factor - tops[p])
            new.append(sums[p] + jnp.sum(w.reshape(-1, 8, wide), axis=0))
            low_w = w.astype(jnp.bfloat16)
            w_ref[0, kb, :, span] = low_w
            ot_scr[:, span] += dot32(value_cols, low_w)
        return tuple(new)

    sums = lax.fori_loop(
        low, high + 1, weigh, tuple(jnp.zeros((8, wide), jnp.float32) for _ in range(pairs))
    )
    for p in range(pairs):
        inverse = 1.0 / jnp.sum(sums[p], axis=0, keepdims=True)
        mixed = ot_scr[:, p * wide : (p + 1) * wide] * inverse
        for i in range(2):
            h = 2 * p + i
            linv_ref[h : h + 1, :] = inverse[:, i * tokens : (i + 1) * tokens]
            columns = lanes((octet * OCTET + h) * HEAD_SIZE, HEAD_SIZE)
            att = mixed[:, i * tokens : (i + 1) * tokens].T.astype(jnp.bfloat16)
            att_ref[:, columns] = att
            hid = (stream_ref[:, columns].astype(jnp.float32) + att.astype(jnp.float32)).astype(
                jnp.bfloat16
            )
            hid_ref[:, columns] = hid
            wide_hid = hid.astype(jnp.float32)
            ss_scr[...] += wide_hid * wide_hid

    @pl.when(octet == pl.num_programs(0) - 1)
    def _():
        mean = jnp.sum(ss_scr[...], axis=1, keepdims=True) * (1.0 / (QUERY_HEADS * HEAD_SIZE))
        inv_rms = jnp.broadcast_to(lax.rsqrt(mean + EPSILON), (tokens, HEAD_SIZE))
        rms_ref[...] = inv_rms

        def norm(h, _):
            columns = lanes(h * HEAD_SIZE, HEAD_SIZE)
            n = (hid_ref[:, columns].astype(jnp.float32) * inv_rms * gain_ref[:, columns]).astype(
                jnp.bfloat16
            )
            norm_ref[:, columns] = n
            rows_scr[pl.ds(h, tokens, stride=PITCH), :] = n.astype(jnp.float32)
            return 0

        lax.fori_loop(0, QUERY_HEADS, norm, 0, unroll=2)
        scatter_rows(slots, rows_scr, send_ref, tokens)


def scatter_rows(slots, rows_scr, send_ref, tokens):
    def send(t, _):
        row = rows_scr[pl.ds(t * PITCH, QUERY_HEADS), :].astype(jnp.bfloat16)
        send_ref[slots[2 * t]] = row
        send_ref[slots[2 * t + 1]] = row
        return 0

    lax.fori_loop(0, tokens, send, 0, unroll=8)


def whole(shape):
    zero = (0,) * len(shape)
    return pl.BlockSpec(shape, lambda *_: zero)


def attend(meta, slots, queries, mine, theirs, stream, gain, slot_count):
    tokens, width = queries.shape
    octets = QUERY_HEADS // OCTET
    blocks = mine.shape[0]
    span = OCTET * tokens
    bf16, f32 = jnp.bfloat16, jnp.float32
    return pl.pallas_call(
        attend_kernel,
        grid_spec=pltpu.PrefetchScalarGridSpec(
            num_scalar_prefetch=2,
            grid=(octets,),
            in_specs=[
                pl.BlockSpec((tokens, OCTET * HEAD_SIZE), lambda o, *_: (0, o)),
                whole(mine.shape),
                whole(theirs.shape),
                whole(stream.shape),
                whole((1, width)),
            ],
            out_specs=[
                pl.BlockSpec((1, blocks, KEY_BLOCK, span), lambda o, *_: (o, 0, 0, 0)),
                pl.BlockSpec((OCTET, tokens), lambda o, *_: (o, 0)),
                whole((tokens, width)),
                whole((tokens, width)),
                whole((tokens, width)),
                whole((tokens, HEAD_SIZE)),
                whole((slot_count, QUERY_HEADS, HEAD_SIZE)),
            ],
            scratch_shapes=[
                pltpu.VMEM((blocks * KEY_BLOCK, mine.shape[2]), bf16),
                pltpu.VMEM((blocks, mine.shape[2] // 2, KEY_BLOCK), bf16),
                pltpu.VMEM((blocks, KEY_BLOCK, tokens), f32),
                pltpu.VMEM((blocks, KEY_BLOCK, span), f32),
                pltpu.VMEM((HEAD_SIZE, span), f32),
                pltpu.VMEM((tokens, HEAD_SIZE), f32),
                pltpu.VMEM((tokens * PITCH, HEAD_SIZE), f32),
            ],
        ),
        out_shape=[
            jax.ShapeDtypeStruct((octets, blocks, KEY_BLOCK, span), bf16),
            jax.ShapeDtypeStruct((QUERY_HEADS, tokens), f32),
            jax.ShapeDtypeStruct((tokens, width), bf16),
            jax.ShapeDtypeStruct((tokens, width), bf16),
            jax.ShapeDtypeStruct((tokens, width), bf16),
            jax.ShapeDtypeStruct((tokens, HEAD_SIZE), f32),
            jax.ShapeDtypeStruct((slot_count, QUERY_HEADS, HEAD_SIZE), bf16),
        ],
        compiler_params=pltpu.CompilerParams(
            dimension_semantics=("arbitrary",), vmem_limit_bytes=VMEM_LIMIT
        ),
        cost_estimate=pl.CostEstimate(
            flops=4 * tokens * width * 1536, bytes_accessed=24 << 20, transcendentals=tokens * 32 * 1536
        ),
        name="attend",
    )(meta, slots, queries, mine, theirs, stream, gain)


def place_kernel(slots, rows_ref, send_ref, rows_scr):
    tokens = rows_ref.shape[0]

    def turn(h, _):
        rows_scr[pl.ds(h, tokens, stride=PITCH), :] = rows_ref[
            :, lanes(h * HEAD_SIZE, HEAD_SIZE)
        ].astype(jnp.float32)
        return 0

    lax.fori_loop(0, QUERY_HEADS, turn, 0, unroll=2)
    scatter_rows(slots, rows_scr, send_ref, tokens)


def place(slots, rows, slot_count):
    tokens, _ = rows.shape
    return pl.pallas_call(
        place_kernel,
        grid_spec=pltpu.PrefetchScalarGridSpec(
            num_scalar_prefetch=1,
            grid=(1,),
            in_specs=[whole(rows.shape)],
            out_specs=whole((slot_count, QUERY_HEADS, HEAD_SIZE)),
            scratch_shapes=[pltpu.VMEM((tokens * PITCH, HEAD_SIZE), jnp.float32)],
        ),
        out_shape=jax.ShapeDtypeStruct((slot_count, QUERY_HEADS, HEAD_SIZE), jnp.bfloat16),
        compiler_params=pltpu.CompilerParams(vmem_limit_bytes=VMEM_LIMIT),
        cost_estimate=pl.CostEstimate(flops=0, bytes_accessed=4 << 20, transcendentals=0),
        name="place",
    )(slots, rows)


def attend_back_kernel(
    meta,
    q_ref,
    grad_ref,
    att_ref,
    linv_ref,
    mine_ref,
    theirs_ref,
    w_ref,
    dq_ref,
    keep_ref,
    give_ref,
    kv_scr,
    kt_scr,
    q_scr,
    do_scr,
    rd_scr,
    ds_scr,
    dqt_scr,
):
    group, step = pl.program_id(0), pl.program_id(1)
    low, high, core = meta[0], meta[1], meta[2]
    tokens = q_ref.shape[0]
    wide = 2 * tokens
    per_group = HEADS_PER_GROUP * tokens
    f32, bf16 = jnp.float32, jnp.bfloat16

    @pl.when((group == 0) & (step == 0))
    def _():
        order_blocks(mine_ref, theirs_ref, core, kv_scr)
        keep_ref[...] = jnp.zeros_like(keep_ref)
        give_ref[...] = jnp.zeros_like(give_ref)

        def prepare(kb, _):
            rows = pl.ds(pl.multiple_of(kb * KEY_BLOCK, KEY_BLOCK), KEY_BLOCK)
            kt_scr[kb] = kv_scr[rows, 0:256].T
            return 0

        lax.fori_loop(low, high + 1, prepare, 0)
        inverse = jnp.concatenate(
            [linv_ref[...], jnp.zeros((128 - QUERY_HEADS, tokens), f32)], axis=0
        ).T
        ones = jnp.ones((8, HEAD_SIZE), bf16)
        for h in range(QUERY_HEADS):
            columns = slice(h * HEAD_SIZE, (h + 1) * HEAD_SIZE)
            rows = slice(h * tokens, (h + 1) * tokens)
            q_scr[rows, :] = q_ref[:, columns]
            scaled = (grad_ref[:, columns].astype(f32) * inverse[:, h : h + 1]).astype(bf16)
            do_scr[rows, :] = scaled
            product = scaled.astype(f32) * att_ref[:, columns].astype(f32)
            head = product.astype(bf16)
            tail = (product - head.astype(f32)).astype(bf16)
            rd_scr[:, rows] = dot32(ones, head, NT) + dot32(ones, tail, NT)

    @pl.when(step == 0)
    def _():
        dqt_scr[...] = jnp.zeros_like(dqt_scr)

    @pl.when(low + step <= high)
    def _():
        kb = low + step
        rows = pl.ds(pl.multiple_of(kb * KEY_BLOCK, KEY_BLOCK), KEY_BLOCK)
        value_rows = kv_scr[rows, lanes(256 + group * HEAD_SIZE, HEAD_SIZE)]
        key_cols = kt_scr[kb, pl.ds(pl.multiple_of(group * HEAD_SIZE, HEAD_SIZE), HEAD_SIZE), :]
        for p in range(HEADS_PER_GROUP // 2):
            here = pl.multiple_of(group * per_group + p * wide, wide)
            grads = do_scr[pl.ds(here, wide), :]
            dp = dot32(value_rows, grads, NT)
            per_octet = OCTET // 2
            c = (p % per_octet) * wide
            w = w_ref[p // per_octet, 0, :, c : c + wide].astype(f32)
            ds = (w * (dp - rd_scr[0:1, pl.ds(here, wide)])).astype(bf16)
            ds_scr[:, p * wide : (p + 1) * wide] = ds
        dqt_scr[...] += dot32(key_cols, ds_scr[...])
        base = pl.multiple_of(group * per_group, per_group)
        half = per_group // 2
        dv = dot32(w_ref[0, 0], do_scr[pl.ds(base, half), :]) + dot32(
            w_ref[1, 0], do_scr[pl.ds(base + half, half), :]
        )
        dk = dot32(ds_scr[...], q_scr[pl.ds(base, per_group), :]) * SCALE
        is_first = jnp.full((128, HEAD_SIZE), core, jnp.int32) == 0
        for part, column in ((dk, 0), (dv, 256)):
            columns = lanes(column + group * HEAD_SIZE, HEAD_SIZE)
            keep_ref[kb, :, columns] = jnp.where(is_first, part[:128], part[128:]).astype(bf16)
            give_ref[kb, :, columns] = jnp.where(is_first, part[128:], part[:128]).astype(bf16)

    @pl.when(step == pl.num_programs(1) - 1)
    def _():
        for h in range(HEADS_PER_GROUP):
            dq = dqt_scr[:, h * tokens : (h + 1) * tokens] * SCALE
            dq_ref[:, lanes(group * per_group + h * HEAD_SIZE, HEAD_SIZE)] = dq.T.astype(bf16)


def attend_back(meta, queries, grads, attended, linv, mine, theirs, weights):
    tokens, width = queries.shape
    blocks = mine.shape[0]
    bf16, f32 = jnp.bfloat16, jnp.float32
    per_group = HEADS_PER_GROUP * tokens
    octets_per_group = HEADS_PER_GROUP // OCTET
    span = OCTET * tokens
    return pl.pallas_call(
        attend_back_kernel,
        grid_spec=pltpu.PrefetchScalarGridSpec(
            num_scalar_prefetch=1,
            grid=(KEY_VALUE_HEADS, blocks),
            in_specs=[
                whole(queries.shape),
                whole(grads.shape),
                whole(attended.shape),
                whole(linv.shape),
                whole(mine.shape),
                whole(theirs.shape),
                pl.BlockSpec(
                    (octets_per_group, 1, KEY_BLOCK, span),
                    lambda g, j, meta: (g, jnp.minimum(meta[0] + j, meta[1]), 0, 0),
                ),
            ],
            out_specs=[whole((tokens, width)), whole(mine.shape), whole(mine.shape)],
            scratch_shapes=[
                pltpu.VMEM((blocks * KEY_BLOCK, mine.shape[2]), bf16),
                pltpu.VMEM((blocks, mine.shape[2] // 2, KEY_BLOCK), bf16),
                pltpu.VMEM((QUERY_HEADS * tokens, HEAD_SIZE), bf16),
                pltpu.VMEM((QUERY_HEADS * tokens, HEAD_SIZE), bf16),
                pltpu.VMEM((8, QUERY_HEADS * tokens), f32),
                pltpu.VMEM((KEY_BLOCK, per_group), bf16),
                pltpu.VMEM((HEAD_SIZE, per_group), f32),
            ],
        ),
        out_shape=[
            jax.ShapeDtypeStruct((tokens, width), bf16),
            jax.ShapeDtypeStruct(mine.shape, bf16),
            jax.ShapeDtypeStruct(mine.shape, bf16),
        ],
        compiler_params=pltpu.CompilerParams(
            dimension_semantics=("arbitrary", "arbitrary"), vmem_limit_bytes=VMEM_LIMIT
        ),
        cost_estimate=pl.CostEstimate(
            flops=8 * tokens * width * 1536, bytes_accessed=20 << 20, transcendentals=0
        ),
        name="attend_back",
    )(meta, queries, grads, attended, linv, mine, theirs, weights)


def expert_kernel(
    rows_ref,
    inner_grad_ref,
    gate_hbm,
    up_hbm,
    out_ref,
    gate_scr,
    up_scr,
    turn_scr,
    x_scr,
    da_scr,
    db_scr,
    score_scr,
    sems,
):
    f32, bf16 = jnp.float32, jnp.bfloat16
    peers, per_peer = rows_ref.shape[0], rows_ref.shape[1]
    count = x_scr.shape[0]
    hidden_units = gate_scr.shape[1]
    capacity = count // peers
    loads = [
        pltpu.make_async_copy(gate_hbm, gate_scr, sems.at[0]),
        pltpu.make_async_copy(up_hbm, up_scr, sems.at[1]),
    ]
    for load in loads:
        load.start()

    def widen(i, _):
        for c in range(capacity):
            row = rows_ref[i, c * QUERY_HEADS : (c + 1) * QUERY_HEADS, :].astype(f32)
            turn_scr[pl.ds((i * capacity + c) * PITCH, QUERY_HEADS), :] = row
        return 0

    lax.fori_loop(0, peers, widen, 0, unroll=2)

    def turn(j, _):
        x_scr[:, lanes(j * HEAD_SIZE, HEAD_SIZE)] = turn_scr[
            pl.ds(j, count, stride=PITCH), :
        ].astype(bf16)
        return 0

    lax.fori_loop(0, QUERY_HEADS, turn, 0, unroll=2)
    for load in loads:
        load.wait()
    score_scr[...] = jnp.zeros_like(score_scr)
    span = 256

    def hidden_part(n, _):
        columns = lanes(n * span, span)
        a = dot32(x_scr[...], gate_scr[:, columns])
        b = dot32(x_scr[...], up_scr[:, columns])
        u = inner_grad_ref[:, columns]
        sig = 1.0 / (1.0 + jnp.exp(-a))
        act = a * sig
        product = u * b
        scores = jnp.sum(product * act, axis=1, keepdims=True)
        score_scr[0:count, :] += jnp.broadcast_to(scores, (count, HEAD_SIZE))
        da_scr[:, columns] = (product * sig * (1.0 + a * (1.0 - sig))).astype(bf16)
        db_scr[:, columns] = (u * act).astype(bf16)
        return 0

    lax.fori_loop(0, hidden_units // span, hidden_part, 0)

    def grad_part(j, _):
        rows = pl.ds(pl.multiple_of(j * span, span), span)
        d = dot32(da_scr[...], gate_scr[rows, :], NT) + dot32(db_scr[...], up_scr[rows, :], NT)
        turn_scr[pl.ds(2 * j, count, stride=PITCH), :] = d[:, :HEAD_SIZE]
        turn_scr[pl.ds(2 * j + 1, count, stride=PITCH), :] = d[:, HEAD_SIZE:]
        return 0

    lax.fori_loop(0, QUERY_HEADS // 2, grad_part, 0)

    def narrow(i, _):
        for c in range(capacity):
            row = turn_scr[pl.ds((i * capacity + c) * PITCH, QUERY_HEADS), :]
            out_ref[i, c * QUERY_HEADS : (c + 1) * QUERY_HEADS, :] = row.astype(bf16)
        out_ref[i, per_peer : per_peer + 8, :] = score_scr[pl.ds(capacity * i, 8), :].astype(bf16)
        return 0

    lax.fori_loop(0, peers, narrow, 0, unroll=2)


def expert(rows, inner_grad, gate_mat, up_mat):
    peers, per_peer, _ = rows.shape
    count = inner_grad.shape[0]
    width, hidden_units = gate_mat.shape
    f32, bf16 = jnp.float32, jnp.bfloat16
    return pl.pallas_call(
        expert_kernel,
        in_specs=[
            pl.BlockSpec(memory_space=pltpu.VMEM),
            pl.BlockSpec(memory_space=pltpu.VMEM),
            pl.BlockSpec(memory_space=pltpu.HBM),
            pl.BlockSpec(memory_space=pltpu.HBM),
        ],
        out_specs=pl.BlockSpec(memory_space=pltpu.VMEM),
        scratch_shapes=[
            pltpu.VMEM((width, hidden_units), bf16),
            pltpu.VMEM((width, hidden_units), bf16),
            pltpu.VMEM((count * PITCH, HEAD_SIZE), f32),
            pltpu.VMEM((count, width), bf16),
            pltpu.VMEM((count, hidden_units), bf16),
            pltpu.VMEM((count, hidden_units), bf16),
            pltpu.VMEM((count + 16, HEAD_SIZE), f32),
            pltpu.SemaphoreType.DMA((2,)),
        ],
        out_shape=jax.ShapeDtypeStruct((peers, per_peer + 8, HEAD_SIZE), bf16),
        compiler_params=pltpu.CompilerParams(vmem_limit_bytes=50 << 20),
        cost_estimate=pl.CostEstimate(
            flops=8 * count * width * hidden_units, bytes_accessed=20 << 20, transcendentals=count * hidden_units
        ),
        name="expert",
    )(rows, inner_grad, gate_mat, up_mat)


def combine_kernel(
    slots,
    gates_smem,
    back_ref,
    gates_ref,
    ids_ref,
    hid_ref,
    norm_ref,
    rms_ref,
    og_ref,
    gain_ref,
    router_ref,
    res_ref,
    part_ref,
    rows_scr,
    score_scr,
    dn_scr,
    acc_scr,
):
    f32, bf16 = jnp.float32, jnp.bfloat16
    tokens = hid_ref.shape[0]
    capacity = 3
    per_peer = capacity * QUERY_HEADS

    def pick(t, _):
        total = None
        scores = []
        for k in range(2):
            slot = slots[2 * t + k]
            e = slot // capacity
            c = slot - e * capacity
            start = pl.multiple_of(c * QUERY_HEADS, QUERY_HEADS)
            row = back_ref[e, pl.ds(start, QUERY_HEADS), :].astype(f32) * gates_smem[2 * t + k]
            total = row if total is None else total + row
            tail = back_ref[e, per_peer : per_peer + 8, :].astype(f32)
            which = lax.broadcasted_iota(jnp.int32, tail.shape, 0) == c
            scores.append(jnp.sum(jnp.where(which, tail, 0.0), axis=0, keepdims=True))
        rows_scr[pl.ds(t * PITCH, QUERY_HEADS), :] = total
        score_scr[pl.ds(t, 1), :] = scores[0] - scores[1]
        return 0

    lax.fori_loop(0, tokens, pick, 0, unroll=8)
    first = gates_ref[:, 0:1]
    value = first * (1.0 - first) * score_scr[...]
    lane = lax.broadcasted_iota(jnp.int32, (tokens, HEAD_SIZE), 1)
    d_logits = jnp.where(lane == ids_ref[:, 0:1], value, 0.0) - jnp.where(
        lane == ids_ref[:, 1:2], value, 0.0
    )
    d_logits = d_logits.astype(bf16)
    acc_scr[...] = jnp.zeros_like(acc_scr)

    def gather(h, _):
        columns = lanes(h * HEAD_SIZE, HEAD_SIZE)
        rows = pl.ds(pl.multiple_of(h * HEAD_SIZE, HEAD_SIZE), HEAD_SIZE)
        dn = rows_scr[pl.ds(h, tokens, stride=PITCH), :] + dot32(
            d_logits, router_ref[rows, :], NT
        )
        scaled = dn * gain_ref[:, columns]
        dn_scr[:, columns] = scaled
        acc_scr[...] += hid_ref[:, columns].astype(f32) * scaled
        part_ref[rows, :] = dot32(norm_ref[:, columns], d_logits, TN).astype(bf16)
        return 0

    lax.fori_loop(0, QUERY_HEADS, gather, 0, unroll=2)
    r = rms_ref[...]
    mean = jnp.sum(acc_scr[...], axis=1, keepdims=True) * (1.0 / (QUERY_HEADS * HEAD_SIZE))
    pull = r * r * r * mean

    def finish(h, _):
        columns = lanes(h * HEAD_SIZE, HEAD_SIZE)
        res = og_ref[:, columns].astype(f32) + r * dn_scr[:, columns] - hid_ref[:, columns].astype(f32) * pull
        res_ref[:, columns] = res.astype(bf16)
        return 0

    lax.fori_loop(0, QUERY_HEADS, finish, 0, unroll=2)


def combine(slots, gates, ids, back, hidden, normed, inv_rms, out_grad, gain, router):
    tokens, width = hidden.shape
    experts = router.shape[1]
    f32, bf16 = jnp.float32, jnp.bfloat16
    return pl.pallas_call(
        combine_kernel,
        in_specs=[pl.BlockSpec(memory_space=pltpu.SMEM)] * 2
        + [pl.BlockSpec(memory_space=pltpu.VMEM)] * 9,
        out_specs=[pl.BlockSpec(memory_space=pltpu.VMEM)] * 2,
        scratch_shapes=[
            pltpu.VMEM((tokens * PITCH, HEAD_SIZE), f32),
            pltpu.VMEM((tokens, HEAD_SIZE), f32),
            pltpu.VMEM((tokens, width), f32),
            pltpu.VMEM((tokens, HEAD_SIZE), f32),
        ],
        out_shape=[
            jax.ShapeDtypeStruct((tokens, width), bf16),
            jax.ShapeDtypeStruct((width, experts), bf16),
        ],
        compiler_params=pltpu.CompilerParams(vmem_limit_bytes=50 << 20),
        cost_estimate=pl.CostEstimate(
            flops=4 * tokens * width * experts, bytes_accessed=9 << 20, transcendentals=0
        ),
        name="combine",
    )(slots, gates.reshape(-1), back, gates, ids, hidden, normed, inv_rms, out_grad, gain, router)


def swap_cores(array):
    return lax.ppermute(array, CORE, [(0, 1), (1, 0)])


def exchange(array, axes):
    return lax.all_to_all(array, axes, split_axis=0, concat_axis=0, tiled=True)


def layer(
    queries,
    keys,
    values,
    stream,
    norm_gain,
    router_weight,
    gate_weight,
    up_weight,
    down_weight,
    doc_lengths,
    expert_ids,
    out_grad,
):
    token_rows = queries.shape[1]
    model_width = queries.shape[2]
    chips = lax.axis_size("blk_0") * lax.axis_size("blk_1")
    core = lax.axis_index(CORE)
    both = jnp.concatenate([keys[0], values[0]], axis=1)
    mine = exchange(jnp.broadcast_to(both[None], (chips, *both.shape)), ZX)
    theirs = swap_cores(mine)

    doc_ends = jnp.cumsum(doc_lengths[0], dtype=jnp.int32)
    first_query = lax.axis_index(BLK) * token_rows
    first_start = jnp.max(jnp.where(doc_ends <= first_query, doc_ends, 0))
    meta = jnp.concatenate(
        [
            jnp.stack(
                [
                    first_start // KEY_BLOCK,
                    (first_query + token_rows - 1) // KEY_BLOCK,
                    core,
                    first_query,
                ]
            ).astype(jnp.int32),
            doc_ends,
        ]
    )
    experts = router_weight.shape[1]
    chosen_ids = expert_ids[0]
    top_count = chosen_ids.shape[1]
    capacity = max(2, 3 * token_rows * top_count // (2 * experts))
    flat_ids = chosen_ids.reshape(-1)
    same = flat_ids[:, None] == flat_ids[None, :]
    order = jnp.arange(flat_ids.shape[0], dtype=jnp.int32)
    slot_rank = jnp.sum((same & (order[None, :] < order[:, None])).astype(jnp.int32), axis=1, dtype=jnp.int32)
    slots = flat_ids * capacity + slot_rank
    slot_count = experts * capacity

    send_grads = place(slots, out_grad[0], slot_count)
    got_grads = exchange(send_grads.reshape(experts, -1, HEAD_SIZE), GRP_BLK)

    weights, linv, attended, hidden, normed, inv_rms, send_rows = attend(
        meta, slots, queries[0], mine, theirs, stream[0], norm_gain[None], slot_count
    )
    got_rows = exchange(send_rows.reshape(experts, -1, HEAD_SIZE), GRP_BLK)

    logits = jnp.dot(normed, router_weight, preferred_element_type=jnp.float32)
    hits = chosen_ids[:, :, None] == jnp.arange(experts, dtype=jnp.int32)[None, None, :]
    chosen = jnp.sum(jnp.where(hits, logits[:, None, :], 0.0), axis=-1)
    first_gate = jax.nn.sigmoid(chosen[:, 0] - chosen[:, 1])
    gates = jnp.stack([first_gate, 1.0 - first_gate], axis=1)

    inner_grad = dot32(got_grads.reshape(slot_count, model_width), down_weight[0], NT)
    back = exchange(expert(got_rows, inner_grad, gate_weight[0], up_weight[0]), GRP_BLK)
    residual_gradient, router_parts = combine(
        slots, gates, chosen_ids, back, hidden, normed, inv_rms, out_grad[0], norm_gain[None], router_weight
    )
    got_parts = exchange(router_parts.reshape(experts, -1, experts), GRP_BLK)
    query_grad, keep, give = attend_back(
        meta, queries[0], residual_gradient, attended, linv, mine, theirs, weights
    )
    pair_sum = (keep.astype(jnp.float32) + swap_cores(give).astype(jnp.float32)).astype(jnp.bfloat16)
    summed = jnp.sum(exchange(pair_sum, ZX).astype(jnp.float32), axis=0).astype(jnp.bfloat16)
    router_grad = jnp.sum(got_parts.astype(jnp.float32), axis=0)
    half = KEY_VALUE_HEADS * HEAD_SIZE
    return (
        query_grad[None],
        summed[None, :, :half],
        summed[None, :, half:],
        residual_gradient[None],
        router_grad,
    )


def solution(mesh):
    split = Mesh(mesh.devices.reshape(2, 4, 4, 2, 2), ("grp_0", "grp_1", "blk_0", "blk_1", "blk_2"))
    return jax.shard_map(
        layer,
        mesh=split,
        in_specs=(
            P(GRP, BLK, None),
            P(GRP, BLK, None),
            P(GRP, BLK, None),
            P(GRP, BLK, None),
            P(),
            P(),
            P(GRP_BLK, None, None),
            P(GRP_BLK, None, None),
            P(GRP_BLK, None, None),
            P(GRP, None),
            P(GRP, BLK, None),
            P(GRP, BLK, None),
        ),
        out_specs=(
            P(GRP, BLK, None),
            P(GRP, BLK, None),
            P(GRP, BLK, None),
            P(GRP, BLK, None),
            P(GRP_BLK, None),
        ),
        check_vma=False,
    )
```

profile of v0, /device:TPU:0, one launch (start us, length us, event | category | flops | bytes accessed | tf_op | source)
XLA Modules:
  0.0 276.2 jit_solution(7180889754373478670)
XLA Ops:
  0.6 0.9 pad_maximum_fusion
  1.5 1.1 broadcast_in_dim.43
  2.6 6.4 %all-to-all-start = ((bf16[8,128,512]{2,1,0:T(8,128)(2,1)}), bf16[8,128,512]{2,1,0:T(8,128)(2,1)S(1)}, u32[]{:S(2)}, u32[]{:S(2)}) async-start(bf16[8,128,512]{2,1,0:T(8,128)(2,1)} %broadcast_in_dim.43), calls=%async_computation | async-start | bytes 2097152 | tf_op jit(solution)/shard_map/all_to_all | solution.py:648
  10.0 4.3 %place.1 = bf16[384,32,128]{2,1,0:T(8,128)(2,1)} custom-call(s32[256]{0:T(256)} %multiply_add_fusion.slots, bf16[128,4096]{1,0:T(8,128)(2,1)} %bitcast.36), custom_call_target="tpu_custom_call" | custom-call | bytes 4194304 | tf_op jit(solution)/shard_map/place/pallas_call | solution.py:265
  14.2 10.4 %all-to-all-done.mine_ref = bf16[8,128,512]{2,1,0:T(8,128)(2,1)S(1)} async-done(((bf16[8,128,512]{2,1,0:T(8,128)(2,1)}), bf16[8,128,512]{2,1,0:T(8,128)(2,1)S(1)}, u32[]{:S(2)}, u32[]{:S(2)}) %all-to-all-start) | async-done | bytes 1048608 | tf_op jit(solution)/shard_map/all_to_all | solution.py:648
  24.6 8.1 %all-to-all-start.2 = ((bf16[128,96,128]{2,1,0:T(8,128)(2,1)}), bf16[128,96,128]{2,1,0:T(8,128)(2,1)}, u32[]{:S(2)}, u32[]{:S(2)}) async-start(bf16[128,96,128]{2,1,0:T(8,128)(2,1)} %bitcast.35), calls=%async_computation.2 | async-start | bytes 6291456 | tf_op jit(solution)/shard_map/all_to_all | solution.py:648
  36.9 1.0 copy-done.8
  37.9 13.8 %attend.1 = (bf16[4,8,256,1024]{3,2,1,0:T(8,128)(2,1)}, f32[32,128]{1,0:T(8,128)}, bf16[128,4096]{1,0:T(8,128)(2,1)}, bf16[128,4096]{1,0:T(8,128)(2,1)}, bf16[12...) custom-call(s32[8]{0:T(128)} %concatenate.6.meta, s32[256]{0:T(256)} %multiply_add_fusion.slots, ...), custom_call_target="tpu_custom_call" | custom-call | flops 3221225472 | bytes 25165824 | tf_op jit(solution)/shard_map/attend/pallas_call | solution.py:200
  51.7 22.2 %all-to-all-done.2 = bf16[128,96,128]{2,1,0:T(8,128)(2,1)} async-done(((bf16[128,96,128]{2,1,0:T(8,128)(2,1)}), bf16[128,96,128]{2,1,0:T(8,128)(2,1)}, u32[]{:S(2)}, u32[]{:S(2)}) %all-to-all-start.2) | async-done | bytes 3145760 | tf_op jit(solution)/shard_map/all_to_all | solution.py:648
  73.9 5.7 %all-to-all-start.1 = ((bf16[128,96,128]{2,1,0:T(8,128)(2,1)}), bf16[128,96,128]{2,1,0:T(8,128)(2,1)}, u32[]{:S(2)}, u32[]{:S(2)}) async-start(bf16[128,96,128]{2,1,0:T(8,128)(2,1)} %bitcast.38), calls=%async_computation.1 | async-start | bytes 6291456 | tf_op jit(solution)/shard_map/all_to_all | solution.py:648
  79.7 5.8 %reshape.62 = bf16[384,4096]{1,0:T(8,128)(2,1)} reshape(bf16[128,96,128]{2,1,0:T(8,128)(2,1)} %all-to-all-done.2) | data formatting | bytes 6291456 | tf_op jit(solution)/shard_map/reshape | solution.py:714
  85.5 6.4 %fusion.inner_grad_ref = f32[384,768]{1,0:T(8,128)S(1)} fusion(bf16[384,4096]{1,0:T(8,128)(2,1)} %reshape.62, bf16[1,768,4096]{2,1,0:T(8,128)(2,1)} %param.20), kind=kOutput, calls=%fused_computation | convolution fusion | flops 2415919104 | bytes 10616832 | tf_op jit(solution)/shard_map/dot_general | solution.py:35
  91.9 29.0 %all-to-all-done.1.rows_ref = bf16[128,96,128]{2,1,0:T(8,128)(2,1)} async-done(((bf16[128,96,128]{2,1,0:T(8,128)(2,1)}), bf16[128,96,128]{2,1,0:T(8,128)(2,1)}, u32[]{:S(2)}, u32[]{:S(2)}) %all-to-all-start.1) | async-done | bytes 3145760 | tf_op jit(solution)/shard_map/all_to_all | solution.py:648
  120.9 23.0 %expert.1 = bf16[128,104,128]{2,1,0:T(8,128)(2,1)} custom-call(bf16[128,96,128]{2,1,0:T(8,128)(2,1)} %all-to-all-done.1.rows_ref, f32[384,768]{1,0:T(8,128)S(1)} %fusion.inner_grad_ref, bf16[4096,768]{1,0:T(8,128)(2,1)} %bitcast.42, bf16[4096,768]{1,0:T(8,128)(2,1)} %bitcast.43), custom_call_target="tpu_custom_call" | custom-call | flops 9663676416 | bytes 20971520 | tf_op jit(solution)/shard_map/expert/pallas_call | solution.py:511
  144.0 6.2 %all-to-all-start.3 = ((bf16[128,104,128]{2,1,0:T(8,128)(2,1)}), bf16[128,104,128]{2,1,0:T(8,128)(2,1)}, u32[]{:S(2)}, u32[]{:S(2)}) async-start(bf16[128,104,128]{2,1,0:T(8,128)(2,1)} %expert.1), calls=%async_computation.3 | async-start | bytes 6815744 | tf_op jit(solution)/shard_map/all_to_all | solution.py:648
  151.2 42.8 %all-to-all-done.3.back_ref = bf16[128,104,128]{2,1,0:T(8,128)(2,1)} async-done(((bf16[128,104,128]{2,1,0:T(8,128)(2,1)}), bf16[128,104,128]{2,1,0:T(8,128)(2,1)}, u32[]{:S(2)}, u32[]{:S(2)}) %all-to-all-start.3) | async-done | bytes 3407904 | tf_op jit(solution)/shard_map/all_to_all | solution.py:648
  194.1 11.2 %combine.1 = (bf16[128,4096]{1,0:T(8,128)(2,1)}, bf16[4096,128]{1,0:T(8,128)(2,1)}) custom-call(s32[256]{0:T(256)S(1)} %copy-done.4, f32[256]{0:T(256)S(1)} %reshape.59.gates_smem, bf16[128,104,128]{2,1,0:T(8,128)(2,1)} %all-to-all-done.3.back_ref, f32[128,2]{1,0:T(8,128)S(1)} %copy.27.gates_ref, s32[128,2]{1,0:T(8,128)S(1)} %bitcast.32, ...), custom_call_target="tpu_custom_call" | custom-call | flops 268435456 | bytes 9437184 | tf_op jit(solution)/shard_map/combine/pallas_call | solution.py:620
  205.3 12.4 %attend_back.1 = (bf16[128,4096]{1,0:T(8,128)(2,1)}, bf16[8,128,512]{2,1,0:T(8,128)(2,1)}, bf16[8,128,512]{2,1,0:T(8,128)(2,1)}) custom-call(s32[8]{0:T(128)} %concatenate.6.meta, bf16[128,4096]{1,0:T(8,128)(2,1)} %bitcast.46, bf16[128,4096]{1,0:T(8,128)(2,1)} %get-tuple-element.21.grad_ref, bf16[128,4096]{1,0:T(8,128)(2,1)} %get-tuple-element.22.att_ref, ...), custom_call_target="tpu_custom_call" | custom-call | flops 6442450944 | bytes 20971520 | tf_op jit(solution)/shard_map/attend_back/pallas_call | solution.py:381
  217.7 19.6 %all-to-all-start.5 = ((bf16[128,32,128]{2,1,0:T(8,128)(2,1)}), bf16[128,32,128]{2,1,0:T(8,128)(2,1)S(1)}, u32[]{:S(2)}, u32[]{:S(2)}) async-start(bf16[128,32,128]{2,1,0:T(8,128)(2,1)} %bitcast.22), calls=%async_computation.5 | async-start | bytes 2097152 | tf_op jit(solution)/shard_map/all_to_all | solution.py:648
  237.3 2.5 add_convert_fusion
  239.8 16.7 %all-to-all-done.5 = bf16[128,32,128]{2,1,0:T(8,128)(2,1)S(1)} async-done(((bf16[128,32,128]{2,1,0:T(8,128)(2,1)}), bf16[128,32,128]{2,1,0:T(8,128)(2,1)S(1)}, u32[]{:S(2)}, u32[]{:S(2)}) %all-to-all-start.5) | async-done | bytes 1048608 | tf_op jit(solution)/shard_map/all_to_all | solution.py:648
  256.5 3.6 %all-to-all-start.4 = ((bf16[8,128,512]{2,1,0:T(8,128)(2,1)}), bf16[8,128,512]{2,1,0:T(8,128)(2,1)S(1)}, u32[]{:S(2)}, u32[]{:S(2)}) async-start(bf16[8,128,512]{2,1,0:T(8,128)(2,1)} %add_convert_fusion), calls=%async_computation.4 | async-start | bytes 2097152 | tf_op jit(solution)/shard_map/all_to_all | solution.py:648
  260.0 0.8 convert_reduce_fusion
  260.8 14.5 %all-to-all-done.4 = bf16[8,128,512]{2,1,0:T(8,128)(2,1)S(1)} async-done(((bf16[8,128,512]{2,1,0:T(8,128)(2,1)}), bf16[8,128,512]{2,1,0:T(8,128)(2,1)S(1)}, u32[]{:S(2)}, u32[]{:S(2)}) %all-to-all-start.4) | async-done | bytes 1048608 | tf_op jit(solution)/shard_map/all_to_all | solution.py:648
  (39 shorter events, 4.4 us)
Async XLA Ops:
  0.6 8.3 %copy-start.7 = (s32[1,128,2]{1,2,0:T(2,128)S(1)}, s32[1,128,2]{1,2,0:T(2,128)}, u32[]{:S(2)}) copy-start(s32[1,128,2]{1,2,0:T(2,128)} %param.22) | copy-start | bytes 3076
  2.6 22.1 %all-to-all-start = ((bf16[8,128,512]{2,1,0:T(8,128)(2,1)}), bf16[8,128,512]{2,1,0:T(8,128)(2,1)S(1)}, u32[]{:S(2)}, u32[]{:S(2)}) async-start(bf16[8,128,512]{2,1,0:T(8,128)(2,1)} %broadcast_in_dim.43), calls=%async_computation | async-start | bytes 2097152 | tf_op jit(solution)/shard_map/all_to_all | solution.py:648
  24.6 8.1 %copy-start.6 = (bf16[8,128,512]{2,1,0:T(8,128)(2,1)}, bf16[8,128,512]{2,1,0:T(8,128)(2,1)S(1)}, u32[]{:S(2)}) copy-start(bf16[8,128,512]{2,1,0:T(8,128)(2,1)S(1)} %all-to-all-done.mine_ref) | copy-start | bytes 3145732
  24.6 8.2 %copy-start.9 = (s32[1,4]{1,0:T(1,128)S(1)}, s32[1,4]{1,0:T(1,128)}, u32[]{:S(2)}) copy-start(s32[1,4]{1,0:T(1,128)} %param.21) | copy-start | bytes 52
  24.6 49.3 %all-to-all-start.2 = ((bf16[128,96,128]{2,1,0:T(8,128)(2,1)}), bf16[128,96,128]{2,1,0:T(8,128)(2,1)}, u32[]{:S(2)}, u32[]{:S(2)}) async-start(bf16[128,96,128]{2,1,0:T(8,128)(2,1)} %bitcast.35), calls=%async_computation.2 | async-start | bytes 6291456 | tf_op jit(solution)/shard_map/all_to_all | solution.py:648
  32.7 4.2 %collective-permute-start = (bf16[8,128,512]{2,1,0:T(8,128)(2,1)S(1)}, bf16[8,128,512]{2,1,0:T(8,128)(2,1)S(1)}, u32[]{:S(2)}, u32[]{:S(2)}) collective-permute-start(bf16[8,128,512]{2,1,0:T(8,128)(2,1)S(1)} %all-to-all-done.mine_ref), channel_id=1, source_target_pairs={{0,1},{1,0},{2,3},{3,2},{4,5},{5,4},{6,7},{7,6},{8,9},{9,8},{10,11... | collective-permute-start | bytes 3145736 | tf_op jit(solution)/shard_map/ppermute | solution.py:644
  36.9 1.0 copy-start.8
  73.9 47.0 %all-to-all-start.1 = ((bf16[128,96,128]{2,1,0:T(8,128)(2,1)}), bf16[128,96,128]{2,1,0:T(8,128)(2,1)}, u32[]{:S(2)}, u32[]{:S(2)}) async-start(bf16[128,96,128]{2,1,0:T(8,128)(2,1)} %bitcast.38), calls=%async_computation.1 | async-start | bytes 6291456 | tf_op jit(solution)/shard_map/all_to_all | solution.py:648
  143.9 6.4 %copy-start = (bf16[128,4096]{1,0:T(8,128)(2,1)S(1)}, bf16[128,4096]{1,0:T(8,128)(2,1)}, u32[]{:S(2)}) copy-start(bf16[128,4096]{1,0:T(8,128)(2,1)} %get-tuple-element.17.norm_ref) | copy-start | bytes 3145732
  143.9 6.4 %copy-start.5 = (bf16[4096,128]{1,0:T(8,128)(2,1)S(1)}, bf16[4096,128]{1,0:T(8,128)(2,1)}, u32[]{:S(2)}) copy-start(bf16[4096,128]{1,0:T(8,128)(2,1)} %router_ref.1) | copy-start | bytes 3145732
  143.9 50.2 %copy-start.1 = (bf16[128,4096]{1,0:T(8,128)(2,1)S(1)}, bf16[128,4096]{1,0:T(8,128)(2,1)}, u32[]{:S(2)}) copy-start(bf16[128,4096]{1,0:T(8,128)(2,1)} %get-tuple-element.19.hid_ref) | copy-start | bytes 3145732
  144.0 50.1 %copy-start.2 = (f32[128,128]{1,0:T(8,128)S(1)}, f32[128,128]{1,0:T(8,128)}, u32[]{:S(2)}) copy-start(f32[128,128]{1,0:T(8,128)} %get-tuple-element.20.rms_ref) | copy-start | bytes 196612
  144.0 50.1 %copy-start.3 = (f32[4096]{0:T(1024)S(1)}, f32[4096]{0:T(1024)}, u32[]{:S(2)}) copy-start(f32[4096]{0:T(1024)} %param.16) | copy-start | bytes 49156
  144.0 50.1 %copy-start.4 = (s32[256]{0:T(256)S(1)}, s32[256]{0:T(256)}, u32[]{:S(2)}) copy-start(s32[256]{0:T(256)} %multiply_add_fusion.slots) | copy-start | bytes 3076
  144.0 50.1 %all-to-all-start.3 = ((bf16[128,104,128]{2,1,0:T(8,128)(2,1)}), bf16[128,104,128]{2,1,0:T(8,128)(2,1)}, u32[]{:S(2)}, u32[]{:S(2)}) async-start(bf16[128,104,128]{2,1,0:T(8,128)(2,1)} %expert.1), calls=%async_computation.3 | async-start | bytes 6815744 | tf_op jit(solution)/shard_map/all_to_all | solution.py:648
  217.7 19.6 %collective-permute-start.1 = (bf16[8,128,512]{2,1,0:T(8,128)(2,1)}, bf16[8,128,512]{2,1,0:T(8,128)(2,1)S(1)}, u32[]{:S(2)}, u32[]{:S(2)}) collective-permute-start(bf16[8,128,512]{2,1,0:T(8,128)(2,1)} %get-tuple-element.27), channel_id=1, source_target_pairs={{0,1},{1,0},{2,3},{3,2},{4,5},{5,4},{6,7},{7,6},{8,9},{9,8},{10,11... | collective-permute-start | bytes 3145736 | tf_op jit(solution)/shard_map/ppermute | solution.py:644
  217.7 38.8 %all-to-all-start.5 = ((bf16[128,32,128]{2,1,0:T(8,128)(2,1)}), bf16[128,32,128]{2,1,0:T(8,128)(2,1)S(1)}, u32[]{:S(2)}, u32[]{:S(2)}) async-start(bf16[128,32,128]{2,1,0:T(8,128)(2,1)} %bitcast.22), calls=%async_computation.5 | async-start | bytes 2097152 | tf_op jit(solution)/shard_map/all_to_all | solution.py:648
  256.5 18.9 %all-to-all-start.4 = ((bf16[8,128,512]{2,1,0:T(8,128)(2,1)}), bf16[8,128,512]{2,1,0:T(8,128)(2,1)S(1)}, u32[]{:S(2)}, u32[]{:S(2)}) async-start(bf16[8,128,512]{2,1,0:T(8,128)(2,1)} %add_convert_fusion), calls=%async_computation.4 | async-start | bytes 2097152 | tf_op jit(solution)/shard_map/all_to_all | solution.py:648
where the time goes:
time: 277 us; the launch traced here: 276 us
  waiting for transfers between devices  136 us (49%)
  Pallas kernels  64.6 us (23%)
  starting transfers between devices  49.6 us (18%)
  local copies, waits for them, and re-layouts  9.82 us (4%)
  matrix products  6.84 us (2%)
  other arithmetic  6.09 us (2%)
  between operations  3.46 us (1%)
    all_to_all x6, waiting for transfers between devices, exchange(): return lax.all_to_all(array, axes, split_axis=0, concat_axis=0, tiled=True)  136 us
    all_to_all x6, starting transfers between devices, exchange(): return lax.all_to_all(array, axes, split_axis=0, concat_axis=0, tiled=True)  49.5 us
    pallas_call x1, Pallas kernels, expert(): pl.pallas_call(expert_kernel, in_specs=[pl.BlockSpec(memory_space=pltpu.V...  23 us
    pallas_call x1, Pallas kernels, attend(): pl.pallas_call(attend_kernel, grid_spec=pltpu.PrefetchScalarGridSpec(num_...  13.8 us
    pallas_call x1, Pallas kernels, attend_back(): pl.pallas_call(attend_back_kernel, grid_spec=pltpu.PrefetchScalarGridSpec...  12.4 us
    pallas_call x1, Pallas kernels, combine(): pl.pallas_call(combine_kernel, in_specs=[pl.BlockSpec(memory_space=pltpu....  11.2 us
    dot_general x1, matrix products, dot32(): return lax.dot_general(a, b, dims, preferred_element_type=jnp.float32)  6.38 us
    reshape x1, local copies, waits for them, and re-layouts, layer(): got_grads.reshape(slot_count, model_width)  5.81 us
  transfers between devices with their start and end apart: 8, of which 6 were waited for; matrix products, arithmetic and copies ran while one was open for 7% of the time, Pallas kernels for 7%

commit v1 on v0

--- a/solution.py
+++ b/solution.py
@@ -37,6 +37,18 @@
 
 def lanes(start, size):
     return pl.ds(pl.multiple_of(start, 128), size)
+
+
+def bounds(meta):
+    place = meta[0] & 15
+    first_query = place * 128
+    ends = [meta[1]]
+    for d in range(1, 4):
+        ends.append(ends[-1] + meta[1 + d])
+    start = jnp.int32(0)
+    for end in ends:
+        start = jnp.where(end <= first_query, end, start)
+    return start // KEY_BLOCK, (first_query + 127) // KEY_BLOCK, meta[0] & 1, first_query, ends
 
 
 def order_blocks(mine_ref, theirs_ref, core, kv_scr):
@@ -78,7 +90,7 @@
 ):
     octet = pl.program_id(0)
     group = octet // (HEADS_PER_GROUP // OCTET)
-    low, high, core, first_query = meta[0], meta[1], meta[2], meta[3]
+    low, high, core, first_query, ends = bounds(meta)
     tokens = q_ref.shape[0]
     factor = SCALE * math.log2(math.e)
 
@@ -89,7 +101,7 @@
         query = first_query + lax.broadcasted_iota(jnp.int32, (KEY_BLOCK, tokens), 1)
         start = jnp.zeros((KEY_BLOCK, tokens), jnp.int32)
         for d in range(4):
-            start = jnp.maximum(start, jnp.where(query >= meta[4 + d], meta[4 + d], 0))
+            start = jnp.maximum(start, jnp.where(query >= ends[d], ends[d], 0))
 
         def prepare(kb, _):
             rows = pl.ds(pl.multiple_of(kb * KEY_BLOCK, KEY_BLOCK), KEY_BLOCK)
@@ -280,13 +292,13 @@
 
 def attend_back_kernel(
     meta,
-    q_ref,
-    grad_ref,
-    att_ref,
+    q_hbm,
+    grad_hbm,
+    att_hbm,
     linv_ref,
-    mine_ref,
-    theirs_ref,
-    w_ref,
+    mine_hbm,
+    theirs_hbm,
+    w_hbm,
     dq_ref,
     keep_ref,
     give_ref,
@@ -297,78 +309,110 @@
     rd_scr,
     ds_scr,
     dqt_scr,
+    w_buf,
+    mine_ref,
+    theirs_ref,
+    q_ref,
+    grad_ref,
+    att_ref,
+    sems,
 ):
-    group, step = pl.program_id(0), pl.program_id(1)
-    low, high, core = meta[0], meta[1], meta[2]
+    operands = ((mine_hbm, mine_ref), (theirs_hbm, theirs_ref), (q_hbm, q_ref), (grad_hbm, grad_ref), (att_hbm, att_ref))
+    loads = [pltpu.make_async_copy(a, b, sems.at[2 + i]) for i, (a, b) in enumerate(operands)]
+    for copy in loads:
+        copy.start()
+    low, high, core, _, _ = bounds(meta)
+    count = high - low + 1
     tokens = q_ref.shape[0]
     wide = 2 * tokens
     per_group = HEADS_PER_GROUP * tokens
+    octets = HEADS_PER_GROUP // OCTET
     f32, bf16 = jnp.float32, jnp.bfloat16
 
-    @pl.when((group == 0) & (step == 0))
-    def _():
-        order_blocks(mine_ref, theirs_ref, core, kv_scr)
-        keep_ref[...] = jnp.zeros_like(keep_ref)
-        give_ref[...] = jnp.zeros_like(give_ref)
-
-        def prepare(kb, _):
+    def load(group, kb, slot):
+        return pltpu.make_async_copy(
+            w_hbm.at[pl.ds(group * octets, octets), kb], w_buf.at[slot], sems.at[slot]
+        )
+
+    load(0, low, 0).start()
+    loads[0].wait()
+    loads[1].wait()
+    order_blocks(mine_ref, theirs_ref, core, kv_scr)
+    keep_ref[...] = jnp.zeros_like(keep_ref)
+    give_ref[...] = jnp.zeros_like(give_ref)
+
+    def prepare(kb, _):
+        rows = pl.ds(pl.multiple_of(kb * KEY_BLOCK, KEY_BLOCK), KEY_BLOCK)
+        kt_scr[kb] = kv_scr[rows, 0:256].T
+        return 0
+
+    lax.fori_loop(low, high + 1, prepare, 0)
+    inverse = jnp.concatenate(
+        [linv_ref[...], jnp.zeros((128 - QUERY_HEADS, tokens), f32)], axis=0
+    ).T
+    ones = jnp.ones((8, HEAD_SIZE), bf16)
+    for copy in loads[2:]:
+        copy.wait()
+    for h in range(QUERY_HEADS):
+        columns = slice(h * HEAD_SIZE, (h + 1) * HEAD_SIZE)
+        rows = slice(h * tokens, (h + 1) * tokens)
+        q_scr[rows, :] = q_ref[:, columns]
+        scaled = (grad_ref[:, columns].astype(f32) * inverse[:, h : h + 1]).astype(bf16)
+        do_scr[rows, :] = scaled
+        product = scaled.astype(f32) * att_ref[:, columns].astype(f32)
+        head = product.astype(bf16)
+        tail = (product - head.astype(f32)).astype(bf16)
+        rd_scr[:, rows] = dot32(ones, head, NT) + dot32(ones, tail, NT)
+
+    is_first = jnp.full((128, HEAD_SIZE), core, jnp.int32) == 0
+
+    def one_group(group, _):
+        dqt_scr[...] = jnp.zeros_like(dqt_scr)
+        base = pl.multiple_of(group * per_group, per_group)
+        half = per_group // octets
+
+        def one_block(j, _):
+            kb = low + j
+            turn = group * count + j
+            slot = lax.rem(turn, 2)
+            load(group, kb, slot).wait()
+
+            @pl.when(turn + 1 < KEY_VALUE_HEADS * count)
+            def _():
+                wrap = j + 1 == count
+                load(
+                    jnp.where(wrap, group + 1, group), low + jnp.where(wrap, 0, j + 1), 1 - slot
+                ).start()
+
             rows = pl.ds(pl.multiple_of(kb * KEY_BLOCK, KEY_BLOCK), KEY_BLOCK)
-            kt_scr[kb] = kv_scr[rows, 0:256].T
+            value_rows = kv_scr[rows, lanes(256 + group * HEAD_SIZE, HEAD_SIZE)]
+            key_cols = kt_scr[kb, pl.ds(pl.multiple_of(group * HEAD_SIZE, HEAD_SIZE), HEAD_SIZE), :]
+            for p in range(HEADS_PER_GROUP // 2):
+                here = pl.multiple_of(group * per_group + p * wide, wide)
+                dp = dot32(value_rows, do_scr[pl.ds(here, wide), :], NT)
+                per_octet = OCTET // 2
+                c = (p % per_octet) * wide
+                w = w_buf[slot, p // per_octet, :, c : c + wide].astype(f32)
+                ds = (w * (dp - rd_scr[0:1, pl.ds(here, wide)])).astype(bf16)
+                ds_scr[:, p * wide : (p + 1) * wide] = ds
+            dqt_scr[...] += dot32(key_cols, ds_scr[...])
+            dv = dot32(w_buf[slot, 0], do_scr[pl.ds(base, half), :]) + dot32(
+                w_buf[slot, 1], do_scr[pl.ds(base + half, half), :]
+            )
+            dk = dot32(ds_scr[...], q_scr[pl.ds(base, per_group), :]) * SCALE
+            for part, column in ((dk, 0), (dv, 256)):
+                columns = lanes(column + group * HEAD_SIZE, HEAD_SIZE)
+                keep_ref[kb, :, columns] = jnp.where(is_first, part[:128], part[128:]).astype(bf16)
+                give_ref[kb, :, columns] = jnp.where(is_first, part[128:], part[:128]).astype(bf16)
             return 0
 
-        lax.fori_loop(low, high + 1, prepare, 0)
-        inverse = jnp.concatenate(
-            [linv_ref[...], jnp.zeros((128 - QUERY_HEADS, tokens), f32)], axis=0
-        ).T
-        ones = jnp.ones((8, HEAD_SIZE), bf16)
-        for h in range(QUERY_HEADS):
-            columns = slice(h * HEAD_SIZE, (h + 1) * HEAD_SIZE)
-            rows = slice(h * tokens, (h + 1) * tokens)
-            q_scr[rows, :] = q_ref[:, columns]
-            scaled = (grad_ref[:, columns].astype(f32) * inverse[:, h : h + 1]).astype(bf16)
-            do_scr[rows, :] = scaled
-            product = scaled.astype(f32) * att_ref[:, columns].astype(f32)
-            head = product.astype(bf16)
-            tail = (product - head.astype(f32)).astype(bf16)
-            rd_scr[:, rows] = dot32(ones, head, NT) + dot32(ones, tail, NT)
-
-    @pl.when(step == 0)
-    def _():
-        dqt_scr[...] = jnp.zeros_like(dqt_scr)
-
-    @pl.when(low + step <= high)
-    def _():
-        kb = low + step
-        rows = pl.ds(pl.multiple_of(kb * KEY_BLOCK, KEY_BLOCK), KEY_BLOCK)
-        value_rows = kv_scr[rows, lanes(256 + group * HEAD_SIZE, HEAD_SIZE)]
-        key_cols = kt_scr[kb, pl.ds(pl.multiple_of(group * HEAD_SIZE, HEAD_SIZE), HEAD_SIZE), :]
-        for p in range(HEADS_PER_GROUP // 2):
-            here = pl.multiple_of(group * per_group + p * wide, wide)
-            grads = do_scr[pl.ds(here, wide), :]
-            dp = dot32(value_rows, grads, NT)
-            per_octet = OCTET // 2
-            c = (p % per_octet) * wide
-            w = w_ref[p // per_octet, 0, :, c : c + wide].astype(f32)
-            ds = (w * (dp - rd_scr[0:1, pl.ds(here, wide)])).astype(bf16)
-            ds_scr[:, p * wide : (p + 1) * wide] = ds
-        dqt_scr[...] += dot32(key_cols, ds_scr[...])
-        base = pl.multiple_of(group * per_group, per_group)
-        half = per_group // 2
-        dv = dot32(w_ref[0, 0], do_scr[pl.ds(base, half), :]) + dot32(
-            w_ref[1, 0], do_scr[pl.ds(base + half, half), :]
-        )
-        dk = dot32(ds_scr[...], q_scr[pl.ds(base, per_group), :]) * SCALE
-        is_first = jnp.full((128, HEAD_SIZE), core, jnp.int32) == 0
-        for part, column in ((dk, 0), (dv, 256)):
-            columns = lanes(column + group * HEAD_SIZE, HEAD_SIZE)
-            keep_ref[kb, :, columns] = jnp.where(is_first, part[:128], part[128:]).astype(bf16)
-            give_ref[kb, :, columns] = jnp.where(is_first, part[128:], part[:128]).astype(bf16)
-
-    @pl.when(step == pl.num_programs(1) - 1)
-    def _():
+        lax.fori_loop(0, count, one_block, 0)
         for h in range(HEADS_PER_GROUP):
             dq = dqt_scr[:, h * tokens : (h + 1) * tokens] * SCALE
             dq_ref[:, lanes(group * per_group + h * HEAD_SIZE, HEAD_SIZE)] = dq.T.astype(bf16)
+        return 0
+
+    lax.fori_loop(0, KEY_VALUE_HEADS, one_group, 0)
 
 
 def attend_back(meta, queries, grads, attended, linv, mine, theirs, weights):
@@ -376,49 +420,96 @@
     blocks = mine.shape[0]
     bf16, f32 = jnp.bfloat16, jnp.float32
     per_group = HEADS_PER_GROUP * tokens
-    octets_per_group = HEADS_PER_GROUP // OCTET
+    octets = HEADS_PER_GROUP // OCTET
     span = OCTET * tokens
+    vmem, hbm = pl.BlockSpec(memory_space=pltpu.VMEM), pl.BlockSpec(memory_space=pltpu.HBM)
     return pl.pallas_call(
         attend_back_kernel,
-        grid_spec=pltpu.PrefetchScalarGridSpec(
-            num_scalar_prefetch=1,
-            grid=(KEY_VALUE_HEADS, blocks),
-            in_specs=[
-                whole(queries.shape),
-                whole(grads.shape),
-                whole(attended.shape),
-                whole(linv.shape),
-                whole(mine.shape),
-                whole(theirs.shape),
-                pl.BlockSpec(
-                    (octets_per_group, 1, KEY_BLOCK, span),
-                    lambda g, j, meta: (g, jnp.minimum(meta[0] + j, meta[1]), 0, 0),
-                ),
-            ],
-            out_specs=[whole((tokens, width)), whole(mine.shape), whole(mine.shape)],
-            scratch_shapes=[
-                pltpu.VMEM((blocks * KEY_BLOCK, mine.shape[2]), bf16),
-                pltpu.VMEM((blocks, mine.shape[2] // 2, KEY_BLOCK), bf16),
-                pltpu.VMEM((QUERY_HEADS * tokens, HEAD_SIZE), bf16),
-                pltpu.VMEM((QUERY_HEADS * tokens, HEAD_SIZE), bf16),
-                pltpu.VMEM((8, QUERY_HEADS * tokens), f32),
-                pltpu.VMEM((KEY_BLOCK, per_group), bf16),
-                pltpu.VMEM((HEAD_SIZE, per_group), f32),
-            ],
-        ),
+        in_specs=[pl.BlockSpec(memory_space=pltpu.SMEM)] + [hbm] * 3 + [vmem] + [hbm] * 3,
+        out_specs=[vmem] * 3,
+        scratch_shapes=[
+            pltpu.VMEM((blocks * KEY_BLOCK, mine.shape[2]), bf16),
+            pltpu.VMEM((blocks, mine.shape[2] // 2, KEY_BLOCK), bf16),
+            pltpu.VMEM((QUERY_HEADS * tokens, HEAD_SIZE), bf16),
+            pltpu.VMEM((QUERY_HEADS * tokens, HEAD_SIZE), bf16),
+            pltpu.VMEM((8, QUERY_HEADS * tokens), f32),
+            pltpu.VMEM((KEY_BLOCK, per_group), bf16),
+            pltpu.VMEM((HEAD_SIZE, per_group), f32),
+            pltpu.VMEM((2, octets, KEY_BLOCK, span), bf16),
+            pltpu.VMEM(mine.shape, bf16),
+            pltpu.VMEM(mine.shape, bf16),
+            pltpu.VMEM((tokens, width), bf16),
+            pltpu.VMEM((tokens, width), bf16),
+            pltpu.VMEM((tokens, width), bf16),
+            pltpu.SemaphoreType.DMA((7,)),
+        ],
         out_shape=[
             jax.ShapeDtypeStruct((tokens, width), bf16),
             jax.ShapeDtypeStruct(mine.shape, bf16),
             jax.ShapeDtypeStruct(mine.shape, bf16),
         ],
-        compiler_params=pltpu.CompilerParams(
-            dimension_semantics=("arbitrary", "arbitrary"), vmem_limit_bytes=VMEM_LIMIT
-        ),
+        compiler_params=pltpu.CompilerParams(vmem_limit_bytes=58 << 20),
         cost_estimate=pl.CostEstimate(
             flops=8 * tokens * width * 1536, bytes_accessed=20 << 20, transcendentals=0
         ),
         name="attend_back",
     )(meta, queries, grads, attended, linv, mine, theirs, weights)
+
+
+def turn_rows(rows_ref, turn_scr, x_scr):
+    peers, per_peer = rows_ref.shape[0], rows_ref.shape[1]
+    capacity = per_peer // QUERY_HEADS
+    count = peers * capacity
+
+    def widen(i, _):
+        for c in range(capacity):
+            row = rows_ref[i, c * QUERY_HEADS : (c + 1) * QUERY_HEADS, :].astype(jnp.float32)
+            turn_scr[pl.ds((i * capacity + c) * PITCH, QUERY_HEADS), :] = row
+        return 0
+
+    lax.fori_loop(0, peers, widen, 0, unroll=2)
+
+    def turn(j, _):
+        x_scr[:, lanes(j * HEAD_SIZE, HEAD_SIZE)] = turn_scr[
+            pl.ds(j, count, stride=PITCH), :
+        ].astype(jnp.bfloat16)
+        return 0
+
+    lax.fori_loop(0, QUERY_HEADS, turn, 0, unroll=2)
+
+
+def down_kernel(rows_ref, down_ref, out_ref, turn_scr, x_scr):
+    turn_rows(rows_ref, turn_scr, x_scr)
+    span = 256
+
+    def part(n, _):
+        rows = pl.ds(pl.multiple_of(n * span, span), span)
+        out_ref[:, lanes(n * span, span)] = dot32(x_scr[...], down_ref[rows, :], NT)
+        return 0
+
+    lax.fori_loop(0, down_ref.shape[0] // span, part, 0)
+
+
+def down(rows, down_mat):
+    peers, per_peer, _ = rows.shape
+    hidden_units, width = down_mat.shape
+    count = peers * per_peer // QUERY_HEADS
+    vmem = pl.BlockSpec(memory_space=pltpu.VMEM)
+    return pl.pallas_call(
+        down_kernel,
+        in_specs=[vmem] * 2,
+        out_specs=vmem,
+        scratch_shapes=[
+            pltpu.VMEM((count * PITCH, HEAD_SIZE), jnp.float32),
+            pltpu.VMEM((count, width), jnp.bfloat16),
+        ],
+        out_shape=jax.ShapeDtypeStruct((count, hidden_units), jnp.float32),
+        compiler_params=pltpu.CompilerParams(vmem_limit_bytes=50 << 20),
+        cost_estimate=pl.CostEstimate(
+            flops=2 * count * width * hidden_units, bytes_accessed=11 << 20, transcendentals=0
+        ),
+        name="down",
+    )(rows, down_mat)
 
 
 def expert_kernel(
@@ -427,8 +518,8 @@
     gate_hbm,
     up_hbm,
     out_ref,
-    gate_scr,
-    up_scr,
+    gate_ref,
+    up_ref,
     turn_scr,
     x_scr,
     da_scr,
@@ -436,42 +527,34 @@
     score_scr,
     sems,
 ):
-    f32, bf16 = jnp.float32, jnp.bfloat16
+    bf16 = jnp.bfloat16
     peers, per_peer = rows_ref.shape[0], rows_ref.shape[1]
     count = x_scr.shape[0]
-    hidden_units = gate_scr.shape[1]
+    hidden_units = gate_ref.shape[1]
     capacity = count // peers
-    loads = [
-        pltpu.make_async_copy(gate_hbm, gate_scr, sems.at[0]),
-        pltpu.make_async_copy(up_hbm, up_scr, sems.at[1]),
-    ]
-    for load in loads:
-        load.start()
-
-    def widen(i, _):
-        for c in range(capacity):
-            row = rows_ref[i, c * QUERY_HEADS : (c + 1) * QUERY_HEADS, :].astype(f32)
-            turn_scr[pl.ds((i * capacity + c) * PITCH, QUERY_HEADS), :] = row
-        return 0
-
-    lax.fori_loop(0, peers, widen, 0, unroll=2)
-
-    def turn(j, _):
-        x_scr[:, lanes(j * HEAD_SIZE, HEAD_SIZE)] = turn_scr[
-            pl.ds(j, count, stride=PITCH), :
-        ].astype(bf16)
-        return 0
-
-    lax.fori_loop(0, QUERY_HEADS, turn, 0, unroll=2)
-    for load in loads:
-        load.wait()
+
+    span = 256
+    parts = hidden_units // span
+
+    def load(n):
+        columns = lanes(n * span, span)
+        return (
+            pltpu.make_async_copy(gate_hbm.at[:, columns], gate_ref.at[:, columns], sems.at[0, n]),
+            pltpu.make_async_copy(up_hbm.at[:, columns], up_ref.at[:, columns], sems.at[1, n]),
+        )
+
+    for n in range(parts):
+        for copy in load(n):
+            copy.start()
+    turn_rows(rows_ref, turn_scr, x_scr)
     score_scr[...] = jnp.zeros_like(score_scr)
-    span = 256
 
     def hidden_part(n, _):
+        for copy in load(n):
+            copy.wait()
         columns = lanes(n * span, span)
-        a = dot32(x_scr[...], gate_scr[:, columns])
-        b = dot32(x_scr[...], up_scr[:, columns])
+        a = dot32(x_scr[...], gate_ref[:, columns])
+        b = dot32(x_scr[...], up_ref[:, columns])
         u = inner_grad_ref[:, columns]
         sig = 1.0 / (1.0 + jnp.exp(-a))
         act = a * sig
@@ -482,11 +565,11 @@
         db_scr[:, columns] = (u * act).astype(bf16)
         return 0
 
-    lax.fori_loop(0, hidden_units // span, hidden_part, 0)
+    lax.fori_loop(0, parts, hidden_part, 0)
 
     def grad_part(j, _):
         rows = pl.ds(pl.multiple_of(j * span, span), span)
-        d = dot32(da_scr[...], gate_scr[rows, :], NT) + dot32(db_scr[...], up_scr[rows, :], NT)
+        d = dot32(da_scr[...], gate_ref[rows, :], NT) + dot32(db_scr[...], up_ref[rows, :], NT)
         turn_scr[pl.ds(2 * j, count, stride=PITCH), :] = d[:, :HEAD_SIZE]
         turn_scr[pl.ds(2 * j + 1, count, stride=PITCH), :] = d[:, HEAD_SIZE:]
         return 0
@@ -510,12 +593,8 @@
     f32, bf16 = jnp.float32, jnp.bfloat16
     return pl.pallas_call(
         expert_kernel,
-        in_specs=[
-            pl.BlockSpec(memory_space=pltpu.VMEM),
-            pl.BlockSpec(memory_space=pltpu.VMEM),
-            pl.BlockSpec(memory_space=pltpu.HBM),
-            pl.BlockSpec(memory_space=pltpu.HBM),
-        ],
+        in_specs=[pl.BlockSpec(memory_space=pltpu.VMEM)] * 2
+        + [pl.BlockSpec(memory_space=pltpu.HBM)] * 2,
         out_specs=pl.BlockSpec(memory_space=pltpu.VMEM),
         scratch_shapes=[
             pltpu.VMEM((width, hidden_units), bf16),
@@ -525,7 +604,7 @@
             pltpu.VMEM((count, hidden_units), bf16),
             pltpu.VMEM((count, hidden_units), bf16),
             pltpu.VMEM((count + 16, HEAD_SIZE), f32),
-            pltpu.SemaphoreType.DMA((2,)),
+            pltpu.SemaphoreType.DMA((2, hidden_units // 256)),
         ],
         out_shape=jax.ShapeDtypeStruct((peers, per_peer + 8, HEAD_SIZE), bf16),
         compiler_params=pltpu.CompilerParams(vmem_limit_bytes=50 << 20),
@@ -537,7 +616,8 @@
 
 
 def combine_kernel(
-    slots,
+    ids_smem,
+    ranks,
     gates_smem,
     back_ref,
     gates_ref,
@@ -564,9 +644,8 @@
         total = None
         scores = []
         for k in range(2):
-            slot = slots[2 * t + k]
-            e = slot // capacity
-            c = slot - e * capacity
+            e = ids_smem[2 * t + k]
+            c = ranks[2 * t + k]
             start = pl.multiple_of(c * QUERY_HEADS, QUERY_HEADS)
             row = back_ref[e, pl.ds(start, QUERY_HEADS), :].astype(f32) * gates_smem[2 * t + k]
             total = row if total is None else total + row
@@ -613,13 +692,13 @@
     lax.fori_loop(0, QUERY_HEADS, finish, 0, unroll=2)
 
 
-def combine(slots, gates, ids, back, hidden, normed, inv_rms, out_grad, gain, router):
+def combine(ranks, gates, ids, back, hidden, normed, inv_rms, out_grad, gain, router):
     tokens, width = hidden.shape
     experts = router.shape[1]
     f32, bf16 = jnp.float32, jnp.bfloat16
     return pl.pallas_call(
         combine_kernel,
-        in_specs=[pl.BlockSpec(memory_space=pltpu.SMEM)] * 2
+        in_specs=[pl.BlockSpec(memory_space=pltpu.SMEM)] * 3
         + [pl.BlockSpec(memory_space=pltpu.VMEM)] * 9,
         out_specs=[pl.BlockSpec(memory_space=pltpu.VMEM)] * 2,
         scratch_shapes=[
@@ -637,7 +716,7 @@
             flops=4 * tokens * width * experts, bytes_accessed=9 << 20, transcendentals=0
         ),
         name="combine",
-    )(slots, gates.reshape(-1), back, gates, ids, hidden, normed, inv_rms, out_grad, gain, router)
+    )(ids.reshape(-1), ranks, gates.reshape(-1), back, gates, ids, hidden, normed, inv_rms, out_grad, gain, router)
 
 
 def swap_cores(array):
@@ -663,29 +742,12 @@
     out_grad,
 ):
     token_rows = queries.shape[1]
-    model_width = queries.shape[2]
     chips = lax.axis_size("blk_0") * lax.axis_size("blk_1")
-    core = lax.axis_index(CORE)
     both = jnp.concatenate([keys[0], values[0]], axis=1)
     mine = exchange(jnp.broadcast_to(both[None], (chips, *both.shape)), ZX)
     theirs = swap_cores(mine)
 
-    doc_ends = jnp.cumsum(doc_lengths[0], dtype=jnp.int32)
-    first_query = lax.axis_index(BLK) * token_rows
-    first_start = jnp.max(jnp.where(doc_ends <= first_query, doc_ends, 0))
-    meta = jnp.concatenate(
-        [
-            jnp.stack(
-                [
-                    first_start // KEY_BLOCK,
-                    (first_query + token_rows - 1) // KEY_BLOCK,
-                    core,
-                    first_query,
-                ]
-            ).astype(jnp.int32),
-            doc_ends,
-        ]
-    )
+    meta = jnp.concatenate([lax.axis_index(GRP_BLK).astype(jnp.int32)[None], doc_lengths[0]])
     experts = router_weight.shape[1]
     chosen_ids = expert_ids[0]
     top_count = chosen_ids.shape[1]
@@ -711,10 +773,10 @@
     first_gate = jax.nn.sigmoid(chosen[:, 0] - chosen[:, 1])
     gates = jnp.stack([first_gate, 1.0 - first_gate], axis=1)
 
-    inner_grad = dot32(got_grads.reshape(slot_count, model_width), down_weight[0], NT)
+    inner_grad = down(got_grads, down_weight[0])
     back = exchange(expert(got_rows, inner_grad, gate_weight[0], up_weight[0]), GRP_BLK)
     residual_gradient, router_parts = combine(
-        slots, gates, chosen_ids, back, hidden, normed, inv_rms, out_grad[0], norm_gain[None], router_weight
+        slot_rank, gates, chosen_ids, back, hidden, normed, inv_rms, out_grad[0], norm_gain[None], router_weight
     )
     got_parts = exchange(router_parts.reshape(experts, -1, experts), GRP_BLK)
     query_grad, keep, give = attend_back(

time: 277 us -> 274 us (0.989)
  waiting for transfers between devices: 136 us -> 145 us
  matrix products: 6.84 us -> 0.44 us
  local copies, waits for them, and re-layouts: 9.82 us -> 4.96 us
    all_to_all x6, waiting for transfers between devices: 136 us -> 142 us  [exchange(): return lax.all_to_all(array, axes, split_axis=0, concat_axis=0, tiled=True)]
    dot_general x1 -> x0, matrix products: 6.38 us -> none  [dot32(): return lax.dot_general(a, b, dims, preferred_element_type=jnp.float32)]
    reshape x1 -> x0, local copies, waits for them, and re-layouts: 5.81 us -> none  [layer(): got_grads.reshape(slot_count, model_width)]
    pallas_call x1 -> x2, Pallas kernels: 12.4 us -> 17.7 us  [the longest x1 9.31 us: attend_back(): pl.pallas_call(attend_back_kernel, in_specs=[pl.BlockSpec(memory_space=pl...]
  transfers between devices with their start and end apart: 8 -> 8, of which waited for: 6 -> 7; matrix products, arithmetic and copies ran while one was open for 7% -> 2% of each run, Pallas kernels for 7% -> 10%
where the time goes in v1:
time: 274 us; the launch traced here: 273 us
  waiting for transfers between devices  145 us (53%)
  Pallas kernels  66.4 us (24%)
  starting transfers between devices  49.7 us (18%)
  other arithmetic  5.88 us (2%)
  local copies, waits for them, and re-layouts  4.96 us (2%)
    all_to_all x6, waiting for transfers between devices, exchange(): return lax.all_to_all(array, axes, split_axis=0, concat_axis=0, tiled=True)  142 us
    all_to_all x6, starting transfers between devices, exchange(): return lax.all_to_all(array, axes, split_axis=0, concat_axis=0, tiled=True)  49.5 us
    pallas_call x1, Pallas kernels, expert(): pl.pallas_call(expert_kernel, in_specs=[pl.BlockSpec(memory_space=pltpu.V...  20.7 us
    pallas_call x1, Pallas kernels, attend(): pl.pallas_call(attend_kernel, grid_spec=pltpu.PrefetchScalarGridSpec(num_...  13.8 us
    pallas_call x1, Pallas kernels, combine(): pl.pallas_call(combine_kernel, in_specs=[pl.BlockSpec(memory_space=pltpu....  9.97 us
    pallas_call x1, Pallas kernels, attend_back(): pl.pallas_call(attend_back_kernel, in_specs=[pl.BlockSpec(memory_space=pl...  9.31 us
    pallas_call x1, Pallas kernels, down(): pl.pallas_call(down_kernel, in_specs=[vmem] * 2, out_specs=vmem, scratch_...  8.35 us
  transfers between devices with their start and end apart: 8, of which 7 were waited for; matrix products, arithmetic and copies ran while one was open for 2% of the time, Pallas kernels for 10%

profile of v1, /device:TPU:0, one launch (start us, length us, event | category | flops | bytes accessed | tf_op | source)
XLA Modules:
  0.0 272.8 jit_solution(9890353605742776947)
XLA Ops:
  0.6 0.9 pad_maximum_fusion
  1.5 1.1 broadcast_in_dim.42
  2.6 6.4 %all-to-all-start = ((bf16[8,128,512]{2,1,0:T(8,128)(2,1)}), bf16[8,128,512]{2,1,0:T(8,128)(2,1)S(1)}, u32[]{:S(2)}, u32[]{:S(2)}) async-start(bf16[8,128,512]{2,1,0:T(8,128)(2,1)} %broadcast_in_dim.42), calls=%async_computation | async-start | bytes 2097152 | tf_op jit(solution)/shard_map/all_to_all | solution.py:727
  10.0 4.3 %place.1 = bf16[384,32,128]{2,1,0:T(8,128)(2,1)} custom-call(s32[256]{0:T(256)} %multiply_add_fusion.slots, bf16[128,4096]{1,0:T(8,128)(2,1)} %bitcast.29), custom_call_target="tpu_custom_call" | custom-call | bytes 4194304 | tf_op jit(solution)/shard_map/place/pallas_call | solution.py:277
  14.3 10.4 %all-to-all-done.mine_ref.mine_hbm = bf16[8,128,512]{2,1,0:T(8,128)(2,1)S(1)} async-done(((bf16[8,128,512]{2,1,0:T(8,128)(2,1)}), bf16[8,128,512]{2,1,0:T(8,128)(2,1)S(1)}, u32[]{:S(2)}, u32[]{:S(2)}) %all-to-all-start) | async-done | bytes 1048608 | tf_op jit(solution)/shard_map/all_to_all | solution.py:727
  24.6 1.0 copy-done.6
  25.6 7.6 %all-to-all-start.2 = ((bf16[128,96,128]{2,1,0:T(8,128)(2,1)}), bf16[128,96,128]{2,1,0:T(8,128)(2,1)S(1)}, u32[]{:S(2)}, u32[]{:S(2)}) async-start(bf16[128,96,128]{2,1,0:T(8,128)(2,1)} %bitcast.27), calls=%async_computation.2 | async-start | bytes 6291456 | tf_op jit(solution)/shard_map/all_to_all | solution.py:727
  33.9 2.4 collective-permute-done.theirs_ref.theirs_hbm
  36.3 13.8 %attend.1 = (bf16[4,8,256,1024]{3,2,1,0:T(8,128)(2,1)}, f32[32,128]{1,0:T(8,128)}, bf16[128,4096]{1,0:T(8,128)(2,1)}, bf16[128,4096]{1,0:T(8,128)(2,1)}, bf16[12...) custom-call(s32[5]{0:T(128)} %pad_add_fusion.meta, s32[256]{0:T(256)} %multiply_add_fusion.slots, ...), custom_call_target="tpu_custom_call" | custom-call | flops 3221225472 | bytes 25165824 | tf_op jit(solution)/shard_map/attend/pallas_call | solution.py:212
  50.1 24.7 %all-to-all-done.2.rows_ref = bf16[128,96,128]{2,1,0:T(8,128)(2,1)S(1)} async-done(((bf16[128,96,128]{2,1,0:T(8,128)(2,1)}), bf16[128,96,128]{2,1,0:T(8,128)(2,1)S(1)}, u32[]{:S(2)}, u32[]{:S(2)}) %all-to-all-start.2) | async-done | bytes 3145760 | tf_op jit(solution)/shard_map/all_to_all | solution.py:727
  74.8 1.7 copy-done.4
  76.5 5.7 %all-to-all-start.1 = ((bf16[128,96,128]{2,1,0:T(8,128)(2,1)}), bf16[128,96,128]{2,1,0:T(8,128)(2,1)}, u32[]{:S(2)}, u32[]{:S(2)}) async-start(bf16[128,96,128]{2,1,0:T(8,128)(2,1)} %bitcast.31), calls=%async_computation.1 | async-start | bytes 6291456 | tf_op jit(solution)/shard_map/all_to_all | solution.py:727
  82.2 8.3 %down.1.inner_grad_ref = f32[384,768]{1,0:T(8,128)S(1)} custom-call(bf16[128,96,128]{2,1,0:T(8,128)(2,1)} %copy-done.4, bf16[768,4096]{1,0:T(8,128)(2,1)} %bitcast.28), custom_call_target="tpu_custom_call" | custom-call | flops 2415919104 | bytes 11534336 | tf_op jit(solution)/shard_map/down/pallas_call | solution.py:498
  90.6 32.9 %all-to-all-done.1.rows_ref = bf16[128,96,128]{2,1,0:T(8,128)(2,1)} async-done(((bf16[128,96,128]{2,1,0:T(8,128)(2,1)}), bf16[128,96,128]{2,1,0:T(8,128)(2,1)}, u32[]{:S(2)}, u32[]{:S(2)}) %all-to-all-start.1) | async-done | bytes 3145760 | tf_op jit(solution)/shard_map/all_to_all | solution.py:727
  123.4 20.7 %expert.1 = bf16[128,104,128]{2,1,0:T(8,128)(2,1)} custom-call(bf16[128,96,128]{2,1,0:T(8,128)(2,1)} %all-to-all-done.1.rows_ref, f32[384,768]{1,0:T(8,128)S(1)} %down.1.inner_grad_ref, bf16[4096,768]{1,0:T(8,128)(2,1)} %bitcast.34, bf16[4096,768]{1,0:T(8,128)(2,1)} %bitcast.35), custom_call_target="tpu_custom_call" | custom-call | flops 9663676416 | bytes 20971520 | tf_op jit(solution)/shard_map/expert/pallas_call | solution.py:594
  144.2 6.0 %all-to-all-start.3 = ((bf16[128,104,128]{2,1,0:T(8,128)(2,1)}), bf16[128,104,128]{2,1,0:T(8,128)(2,1)}, u32[]{:S(2)}, u32[]{:S(2)}) async-start(bf16[128,104,128]{2,1,0:T(8,128)(2,1)} %expert.1), calls=%async_computation.3 | async-start | bytes 6815744 | tf_op jit(solution)/shard_map/all_to_all | solution.py:727
  151.3 43.0 %all-to-all-done.3.back_ref = bf16[128,104,128]{2,1,0:T(8,128)(2,1)} async-done(((bf16[128,104,128]{2,1,0:T(8,128)(2,1)}), bf16[128,104,128]{2,1,0:T(8,128)(2,1)}, u32[]{:S(2)}, u32[]{:S(2)}) %all-to-all-start.3) | async-done | bytes 3407904 | tf_op jit(solution)/shard_map/all_to_all | solution.py:727
  194.3 10.0 %combine.1 = (bf16[128,4096]{1,0:T(8,128)(2,1)}, bf16[4096,128]{1,0:T(8,128)(2,1)}) custom-call(s32[256]{0:T(256)S(1)} %reshape_squeeze.4.ids_smem, s32[256]{0:T(256)S(1)} %convert_reduce_fusion.1.ranks, f32[256]{0:T(256)S(1)} %reshape.27.gates_smem, bf16[128,104,128]{2,1,0:T(8,128)(2,1)} %all-to-all-done.3.back_ref, f32[128,2]{1,0:T(8,128)S(1)} %copy.27.gates_ref, ...), custom_call_target="tpu_custom_call" | custom-call | flops 268435456 | bytes 9437184 | tf_op jit(solution)/shard_map/combine/pallas_call | solution.py:699
  204.3 9.3 %attend_back.1 = (bf16[128,4096]{1,0:T(8,128)(2,1)}, bf16[8,128,512]{2,1,0:T(8,128)(2,1)}, bf16[8,128,512]{2,1,0:T(8,128)(2,1)}) custom-call(s32[5]{0:T(128)} %pad_add_fusion.meta, bf16[128,4096]{1,0:T(8,128)(2,1)} %bitcast.38, bf16[128,4096]{1,0:T(8,128)(2,1)} %get-tuple-element.21.grad_hbm, bf16[128,4096]{1,0:T(8,128)(2,1)} %get-tuple-element.22.att_hbm, ...), custom_call_target="tpu_custom_call" | custom-call | flops 6442450944 | bytes 20971520 | tf_op jit(solution)/shard_map/attend_back/pallas_call | solution.py:426
  213.7 20.2 %all-to-all-start.5 = ((bf16[128,32,128]{2,1,0:T(8,128)(2,1)}), bf16[128,32,128]{2,1,0:T(8,128)(2,1)S(1)}, u32[]{:S(2)}, u32[]{:S(2)}) async-start(bf16[128,32,128]{2,1,0:T(8,128)(2,1)} %bitcast.18), calls=%async_computation.5 | async-start | bytes 2097152 | tf_op jit(solution)/shard_map/all_to_all | solution.py:727
  234.0 2.5 add_convert_fusion
  236.5 16.7 %all-to-all-done.5 = bf16[128,32,128]{2,1,0:T(8,128)(2,1)S(1)} async-done(((bf16[128,32,128]{2,1,0:T(8,128)(2,1)}), bf16[128,32,128]{2,1,0:T(8,128)(2,1)S(1)}, u32[]{:S(2)}, u32[]{:S(2)}) %all-to-all-start.5) | async-done | bytes 1048608 | tf_op jit(solution)/shard_map/all_to_all | solution.py:727
  253.1 3.6 %all-to-all-start.4 = ((bf16[8,128,512]{2,1,0:T(8,128)(2,1)}), bf16[8,128,512]{2,1,0:T(8,128)(2,1)S(1)}, u32[]{:S(2)}, u32[]{:S(2)}) async-start(bf16[8,128,512]{2,1,0:T(8,128)(2,1)} %add_convert_fusion), calls=%async_computation.4 | async-start | bytes 2097152 | tf_op jit(solution)/shard_map/all_to_all | solution.py:727
  257.5 14.5 %all-to-all-done.4 = bf16[8,128,512]{2,1,0:T(8,128)(2,1)S(1)} async-done(((bf16[8,128,512]{2,1,0:T(8,128)(2,1)}), bf16[8,128,512]{2,1,0:T(8,128)(2,1)S(1)}, u32[]{:S(2)}, u32[]{:S(2)}) %all-to-all-start.4) | async-done | bytes 1048608 | tf_op jit(solution)/shard_map/all_to_all | solution.py:727
  (34 shorter events, 4.4 us)
Async XLA Ops:
  0.6 8.3 %copy-start.7 = (s32[1,128,2]{1,2,0:T(2,128)S(1)}, s32[1,128,2]{1,2,0:T(2,128)}, u32[]{:S(2)}) copy-start(s32[1,128,2]{1,2,0:T(2,128)} %param.22) | copy-start | bytes 3076
  2.6 22.1 %all-to-all-start = ((bf16[8,128,512]{2,1,0:T(8,128)(2,1)}), bf16[8,128,512]{2,1,0:T(8,128)(2,1)S(1)}, u32[]{:S(2)}, u32[]{:S(2)}) async-start(bf16[8,128,512]{2,1,0:T(8,128)(2,1)} %broadcast_in_dim.42), calls=%async_computation | async-start | bytes 2097152 | tf_op jit(solution)/shard_map/all_to_all | solution.py:727
  24.6 1.0 copy-start.6
  24.6 8.7 %copy-start.8 = (s32[1,4]{1,0:T(1,128)S(1)}, s32[1,4]{1,0:T(1,128)}, u32[]{:S(2)}) copy-start(s32[1,4]{1,0:T(1,128)} %param.21) | copy-start | bytes 52
  25.6 49.2 %all-to-all-start.2 = ((bf16[128,96,128]{2,1,0:T(8,128)(2,1)}), bf16[128,96,128]{2,1,0:T(8,128)(2,1)S(1)}, u32[]{:S(2)}, u32[]{:S(2)}) async-start(bf16[128,96,128]{2,1,0:T(8,128)(2,1)} %bitcast.27), calls=%async_computation.2 | async-start | bytes 6291456 | tf_op jit(solution)/shard_map/all_to_all | solution.py:727
  33.2 3.1 %collective-permute-start = (bf16[8,128,512]{2,1,0:T(8,128)(2,1)}, bf16[8,128,512]{2,1,0:T(8,128)(2,1)}, u32[]{:S(2)}, u32[]{:S(2)}) collective-permute-start(bf16[8,128,512]{2,1,0:T(8,128)(2,1)} %copy-done.6), channel_id=1, source_target_pairs={{0,1},{1,0},{2,3},{3,2},{4,5},{5,4},{6,7},{7,6},{8,9},{9,8},{10,11... | collective-permute-start | bytes 3145736 | tf_op jit(solution)/shard_map/ppermute | solution.py:723
  74.8 1.7 copy-start.4
  76.5 47.0 %all-to-all-start.1 = ((bf16[128,96,128]{2,1,0:T(8,128)(2,1)}), bf16[128,96,128]{2,1,0:T(8,128)(2,1)}, u32[]{:S(2)}, u32[]{:S(2)}) async-start(bf16[128,96,128]{2,1,0:T(8,128)(2,1)} %bitcast.31), calls=%async_computation.1 | async-start | bytes 6291456 | tf_op jit(solution)/shard_map/all_to_all | solution.py:727
  144.2 6.2 %copy-start = (bf16[128,4096]{1,0:T(8,128)(2,1)S(1)}, bf16[128,4096]{1,0:T(8,128)(2,1)}, u32[]{:S(2)}) copy-start(bf16[128,4096]{1,0:T(8,128)(2,1)} %get-tuple-element.17.norm_ref) | copy-start | bytes 3145732
  144.2 6.2 %copy-start.5 = (bf16[4096,128]{1,0:T(8,128)(2,1)S(1)}, bf16[4096,128]{1,0:T(8,128)(2,1)}, u32[]{:S(2)}) copy-start(bf16[4096,128]{1,0:T(8,128)(2,1)} %router_ref.1) | copy-start | bytes 3145732
  144.2 50.1 %copy-start.1 = (bf16[128,4096]{1,0:T(8,128)(2,1)S(1)}, bf16[128,4096]{1,0:T(8,128)(2,1)}, u32[]{:S(2)}) copy-start(bf16[128,4096]{1,0:T(8,128)(2,1)} %get-tuple-element.19.hid_ref) | copy-start | bytes 3145732
  144.2 50.1 %copy-start.2 = (f32[128,128]{1,0:T(8,128)S(1)}, f32[128,128]{1,0:T(8,128)}, u32[]{:S(2)}) copy-start(f32[128,128]{1,0:T(8,128)} %get-tuple-element.20.rms_ref) | copy-start | bytes 196612
  144.2 50.1 %copy-start.3 = (f32[4096]{0:T(1024)S(1)}, f32[4096]{0:T(1024)}, u32[]{:S(2)}) copy-start(f32[4096]{0:T(1024)} %param.16) | copy-start | bytes 49156
  144.2 50.1 %all-to-all-start.3 = ((bf16[128,104,128]{2,1,0:T(8,128)(2,1)}), bf16[128,104,128]{2,1,0:T(8,128)(2,1)}, u32[]{:S(2)}, u32[]{:S(2)}) async-start(bf16[128,104,128]{2,1,0:T(8,128)(2,1)} %expert.1), calls=%async_computation.3 | async-start | bytes 6815744 | tf_op jit(solution)/shard_map/all_to_all | solution.py:727
  213.6 20.3 %collective-permute-start.1 = (bf16[8,128,512]{2,1,0:T(8,128)(2,1)}, bf16[8,128,512]{2,1,0:T(8,128)(2,1)S(1)}, u32[]{:S(2)}, u32[]{:S(2)}) collective-permute-start(bf16[8,128,512]{2,1,0:T(8,128)(2,1)} %get-tuple-element.27), channel_id=1, source_target_pairs={{0,1},{1,0},{2,3},{3,2},{4,5},{5,4},{6,7},{7,6},{8,9},{9,8},{10,11... | collective-permute-start | bytes 3145736 | tf_op jit(solution)/shard_map/ppermute | solution.py:723
  213.7 39.4 %all-to-all-start.5 = ((bf16[128,32,128]{2,1,0:T(8,128)(2,1)}), bf16[128,32,128]{2,1,0:T(8,128)(2,1)S(1)}, u32[]{:S(2)}, u32[]{:S(2)}) async-start(bf16[128,32,128]{2,1,0:T(8,128)(2,1)} %bitcast.18), calls=%async_computation.5 | async-start | bytes 2097152 | tf_op jit(solution)/shard_map/all_to_all | solution.py:727
  253.1 18.9 %all-to-all-start.4 = ((bf16[8,128,512]{2,1,0:T(8,128)(2,1)}), bf16[8,128,512]{2,1,0:T(8,128)(2,1)S(1)}, u32[]{:S(2)}, u32[]{:S(2)}) async-start(bf16[8,128,512]{2,1,0:T(8,128)(2,1)} %add_convert_fusion), calls=%async_computation.4 | async-start | bytes 2097152 | tf_op jit(solution)/shard_map/all_to_all | solution.py:727

commit v2 on v1

--- a/solution.py
+++ b/solution.py
@@ -51,26 +51,29 @@
     return start // KEY_BLOCK, (first_query + 127) // KEY_BLOCK, meta[0] & 1, first_query, ends
 
 
-def order_blocks(mine_ref, theirs_ref, core, kv_scr):
-    is_first = jnp.full((128, mine_ref.shape[2]), core, jnp.int32) == 0
-
-    def place(b, _):
-        mine = mine_ref[b].astype(jnp.float32)
-        theirs = theirs_ref[b].astype(jnp.float32)
-        start = pl.multiple_of(b * KEY_BLOCK, KEY_BLOCK)
-        kv_scr[pl.ds(start, 128), :] = jnp.where(is_first, mine, theirs).astype(jnp.bfloat16)
-        kv_scr[pl.ds(start + 128, 128), :] = jnp.where(is_first, theirs, mine).astype(jnp.bfloat16)
-        return 0
-
-    lax.fori_loop(0, mine_ref.shape[0], place, 0)
+def block_loads(meta, sources, kv_scr, sems):
+    core, x = meta[0] & 1, (meta[0] >> 1) & 1
+    copies = []
+    for i, source in enumerate(sources):
+        for z in range(source.shape[0]):
+            block = (z * 2 + ((x + i) & 1)) * 2 + ((core + i // 2) & 1)
+            rows = pl.ds(pl.multiple_of(block * 128, 128), 128)
+            copies.append(
+                pltpu.make_async_copy(
+                    source.at[z], kv_scr.at[rows, :], sems.at[i * source.shape[0] + z]
+                )
+            )
+    return copies
 
 
 def attend_kernel(
     meta,
     slots,
     q_ref,
-    mine_ref,
-    theirs_ref,
+    near_hbm,
+    far_hbm,
+    near_other_hbm,
+    far_other_hbm,
     stream_ref,
     gain_ref,
     w_ref,
@@ -87,21 +90,28 @@
     ot_scr,
     ss_scr,
     rows_scr,
+    sems,
 ):
     octet = pl.program_id(0)
     group = octet // (HEADS_PER_GROUP // OCTET)
-    low, high, core, first_query, ends = bounds(meta)
+    low, high, _, first_query, ends = bounds(meta)
     tokens = q_ref.shape[0]
     factor = SCALE * math.log2(math.e)
 
     @pl.when(octet == 0)
     def _():
-        order_blocks(mine_ref, theirs_ref, core, kv_scr)
+        sources = (near_hbm, far_hbm, near_other_hbm, far_other_hbm)
+        copies = block_loads(meta, sources, kv_scr, sems)
+        for copy in copies:
+            copy.start()
         ss_scr[...] = jnp.zeros_like(ss_scr)
         query = first_query + lax.broadcasted_iota(jnp.int32, (KEY_BLOCK, tokens), 1)
         start = jnp.zeros((KEY_BLOCK, tokens), jnp.int32)
         for d in range(4):
             start = jnp.maximum(start, jnp.where(query >= ends[d], ends[d], 0))
+
+        for copy in copies:
+            copy.wait()
 
         def prepare(kb, _):
             rows = pl.ds(pl.multiple_of(kb * KEY_BLOCK, KEY_BLOCK), KEY_BLOCK)
@@ -203,10 +213,11 @@
     return pl.BlockSpec(shape, lambda *_: zero)
 
 
-def attend(meta, slots, queries, mine, theirs, stream, gain, slot_count):
+def attend(meta, slots, queries, sources, stream, gain, slot_count):
     tokens, width = queries.shape
     octets = QUERY_HEADS // OCTET
-    blocks = mine.shape[0]
+    blocks = 2 * sources[0].shape[0]
+    columns = sources[0].shape[2]
     span = OCTET * tokens
     bf16, f32 = jnp.bfloat16, jnp.float32
     return pl.pallas_call(
@@ -216,8 +227,7 @@
             grid=(octets,),
             in_specs=[
                 pl.BlockSpec((tokens, OCTET * HEAD_SIZE), lambda o, *_: (0, o)),
-                whole(mine.shape),
-                whole(theirs.shape),
+                *[pl.BlockSpec(memory_space=pltpu.HBM)] * 4,
                 whole(stream.shape),
                 whole((1, width)),
             ],
@@ -231,13 +241,14 @@
                 whole((slot_count, QUERY_HEADS, HEAD_SIZE)),
             ],
             scratch_shapes=[
-                pltpu.VMEM((blocks * KEY_BLOCK, mine.shape[2]), bf16),
-                pltpu.VMEM((blocks, mine.shape[2] // 2, KEY_BLOCK), bf16),
+                pltpu.VMEM((blocks * KEY_BLOCK, columns), bf16),
+                pltpu.VMEM((blocks, columns // 2, KEY_BLOCK), bf16),
                 pltpu.VMEM((blocks, KEY_BLOCK, tokens), f32),
                 pltpu.VMEM((blocks, KEY_BLOCK, span), f32),
                 pltpu.VMEM((HEAD_SIZE, span), f32),
                 pltpu.VMEM((tokens, HEAD_SIZE), f32),
                 pltpu.VMEM((tokens * PITCH, HEAD_SIZE), f32),
+                pltpu.SemaphoreType.DMA((16,)),
             ],
         ),
         out_shape=[
@@ -256,7 +267,7 @@
             flops=4 * tokens * width * 1536, bytes_accessed=24 << 20, transcendentals=tokens * 32 * 1536
         ),
         name="attend",
-    )(meta, slots, queries, mine, theirs, stream, gain)
+    )(meta, slots, queries, *sources, stream, gain)
 
 
 def place_kernel(slots, rows_ref, send_ref, rows_scr):
@@ -296,8 +307,10 @@
     grad_hbm,
     att_hbm,
     linv_ref,
-    mine_hbm,
-    theirs_hbm,
+    near_hbm,
+    far_hbm,
+    near_other_hbm,
+    far_other_hbm,
     w_hbm,
     dq_ref,
     keep_ref,
@@ -310,14 +323,19 @@
     ds_scr,
     dqt_scr,
     w_buf,
-    mine_ref,
-    theirs_ref,
     q_ref,
     grad_ref,
     att_ref,
     sems,
+    block_sems,
 ):
-    operands = ((mine_hbm, mine_ref), (theirs_hbm, theirs_ref), (q_hbm, q_ref), (grad_hbm, grad_ref), (att_hbm, att_ref))
+    blocks = block_loads(
+        meta, (near_hbm, far_hbm, near_other_hbm, far_other_hbm), kv_scr, block_sems
+    )
+    for copy in blocks:
+        copy.start()
+
+    operands = ((q_hbm, q_ref), (grad_hbm, grad_ref), (att_hbm, att_ref))
     loads = [pltpu.make_async_copy(a, b, sems.at[2 + i]) for i, (a, b) in enumerate(operands)]
     for copy in loads:
         copy.start()
@@ -335,11 +353,10 @@
         )
 
     load(0, low, 0).start()
-    loads[0].wait()
-    loads[1].wait()
-    order_blocks(mine_ref, theirs_ref, core, kv_scr)
     keep_ref[...] = jnp.zeros_like(keep_ref)
     give_ref[...] = jnp.zeros_like(give_ref)
+    for copy in blocks:
+        copy.wait()
 
     def prepare(kb, _):
         rows = pl.ds(pl.multiple_of(kb * KEY_BLOCK, KEY_BLOCK), KEY_BLOCK)
@@ -351,7 +368,7 @@
         [linv_ref[...], jnp.zeros((128 - QUERY_HEADS, tokens), f32)], axis=0
     ).T
     ones = jnp.ones((8, HEAD_SIZE), bf16)
-    for copy in loads[2:]:
+    for copy in loads:
         copy.wait()
     for h in range(QUERY_HEADS):
         columns = slice(h * HEAD_SIZE, (h + 1) * HEAD_SIZE)
@@ -415,9 +432,11 @@
     lax.fori_loop(0, KEY_VALUE_HEADS, one_group, 0)
 
 
-def attend_back(meta, queries, grads, attended, linv, mine, theirs, weights):
+def attend_back(meta, queries, grads, attended, linv, sources, weights):
     tokens, width = queries.shape
-    blocks = mine.shape[0]
+    blocks = 2 * sources[0].shape[0]
+    columns = sources[0].shape[2]
+    parts = (blocks, 128, columns)
     bf16, f32 = jnp.bfloat16, jnp.float32
     per_group = HEADS_PER_GROUP * tokens
     octets = HEADS_PER_GROUP // OCTET
@@ -425,35 +444,34 @@
     vmem, hbm = pl.BlockSpec(memory_space=pltpu.VMEM), pl.BlockSpec(memory_space=pltpu.HBM)
     return pl.pallas_call(
         attend_back_kernel,
-        in_specs=[pl.BlockSpec(memory_space=pltpu.SMEM)] + [hbm] * 3 + [vmem] + [hbm] * 3,
+        in_specs=[pl.BlockSpec(memory_space=pltpu.SMEM)] + [hbm] * 3 + [vmem] + [hbm] * 5,
         out_specs=[vmem] * 3,
         scratch_shapes=[
-            pltpu.VMEM((blocks * KEY_BLOCK, mine.shape[2]), bf16),
-            pltpu.VMEM((blocks, mine.shape[2] // 2, KEY_BLOCK), bf16),
+            pltpu.VMEM((blocks * KEY_BLOCK, columns), bf16),
+            pltpu.VMEM((blocks, columns // 2, KEY_BLOCK), bf16),
             pltpu.VMEM((QUERY_HEADS * tokens, HEAD_SIZE), bf16),
             pltpu.VMEM((QUERY_HEADS * tokens, HEAD_SIZE), bf16),
             pltpu.VMEM((8, QUERY_HEADS * tokens), f32),
             pltpu.VMEM((KEY_BLOCK, per_group), bf16),
             pltpu.VMEM((HEAD_SIZE, per_group), f32),
             pltpu.VMEM((2, octets, KEY_BLOCK, span), bf16),
-            pltpu.VMEM(mine.shape, bf16),
-            pltpu.VMEM(mine.shape, bf16),
             pltpu.VMEM((tokens, width), bf16),
             pltpu.VMEM((tokens, width), bf16),
             pltpu.VMEM((tokens, width), bf16),
-            pltpu.SemaphoreType.DMA((7,)),
+            pltpu.SemaphoreType.DMA((5,)),
+            pltpu.SemaphoreType.DMA((16,)),
         ],
         out_shape=[
             jax.ShapeDtypeStruct((tokens, width), bf16),
-            jax.ShapeDtypeStruct(mine.shape, bf16),
-            jax.ShapeDtypeStruct(mine.shape, bf16),
+            jax.ShapeDtypeStruct(parts, bf16),
+            jax.ShapeDtypeStruct(parts, bf16),
         ],
         compiler_params=pltpu.CompilerParams(vmem_limit_bytes=58 << 20),
         cost_estimate=pl.CostEstimate(
             flops=8 * tokens * width * 1536, bytes_accessed=20 << 20, transcendentals=0
         ),
         name="attend_back",
-    )(meta, queries, grads, attended, linv, mine, theirs, weights)
+    )(meta, queries, grads, attended, linv, *sources, weights)
 
 
 def turn_rows(rows_ref, turn_scr, x_scr):
@@ -504,7 +522,7 @@
             pltpu.VMEM((count, width), jnp.bfloat16),
         ],
         out_shape=jax.ShapeDtypeStruct((count, hidden_units), jnp.float32),
-        compiler_params=pltpu.CompilerParams(vmem_limit_bytes=50 << 20),
+        compiler_params=pltpu.CompilerParams(vmem_limit_bytes=24 << 20),
         cost_estimate=pl.CostEstimate(
             flops=2 * count * width * hidden_units, bytes_accessed=11 << 20, transcendentals=0
         ),
@@ -742,10 +760,11 @@
     out_grad,
 ):
     token_rows = queries.shape[1]
-    chips = lax.axis_size("blk_0") * lax.axis_size("blk_1")
     both = jnp.concatenate([keys[0], values[0]], axis=1)
-    mine = exchange(jnp.broadcast_to(both[None], (chips, *both.shape)), ZX)
-    theirs = swap_cores(mine)
+    near = exchange(jnp.broadcast_to(both[None], (lax.axis_size("blk_0"), *both.shape)), "blk_0")
+    far = lax.ppermute(near, "blk_1", [(0, 1), (1, 0)])
+    near_other = swap_cores(near)
+    sources = (near, far, near_other, swap_cores(far))
 
     meta = jnp.concatenate([lax.axis_index(GRP_BLK).astype(jnp.int32)[None], doc_lengths[0]])
     experts = router_weight.shape[1]
@@ -763,7 +782,7 @@
     got_grads = exchange(send_grads.reshape(experts, -1, HEAD_SIZE), GRP_BLK)
 
     weights, linv, attended, hidden, normed, inv_rms, send_rows = attend(
-        meta, slots, queries[0], mine, theirs, stream[0], norm_gain[None], slot_count
+        meta, slots, queries[0], sources, stream[0], norm_gain[None], slot_count
     )
     got_rows = exchange(send_rows.reshape(experts, -1, HEAD_SIZE), GRP_BLK)
 
@@ -780,7 +799,7 @@
     )
     got_parts = exchange(router_parts.reshape(experts, -1, experts), GRP_BLK)
     query_grad, keep, give = attend_back(
-        meta, queries[0], residual_gradient, attended, linv, mine, theirs, weights
+        meta, queries[0], residual_gradient, attended, linv, sources, weights
     )
     pair_sum = (keep.astype(jnp.float32) + swap_cores(give).astype(jnp.float32)).astype(jnp.bfloat16)
     summed = jnp.sum(exchange(pair_sum, ZX).astype(jnp.float32), axis=0).astype(jnp.bfloat16)

time: 274 us -> 309 us (1.13)
  starting transfers between devices: 49.7 us -> 70.3 us
  waiting for transfers between devices: 145 us -> 156 us
  local copies, waits for them, and re-layouts: 4.96 us -> 8.68 us
    ppermute x0 -> x1, waiting for transfers between devices: none -> 45.3 us  [layer(): far = lax.ppermute(near, 'blk_1', [(0, 1), (1, 0)])]
    all_to_all x6, waiting for transfers between devices: 142 us -> 109 us  [exchange(): return lax.all_to_all(array, axes, split_axis=0, concat_axis=0, tiled=True)]
    all_to_all x6, starting transfers between devices: 49.5 us -> 69.2 us  [exchange(): return lax.all_to_all(array, axes, split_axis=0, concat_axis=0, tiled=True)]
    unnamed x19, local copies, waits for them, and re-layouts: 2.78 us -> 6.74 us
    pallas_call x1, Pallas kernels: 8.35 us -> 4.63 us  [down(): pl.pallas_call(down_kernel, in_specs=[vmem] * 2, out_specs=vmem, scratch_...]
  transfers between devices with their start and end apart: 8 -> 10, of which waited for: 7 -> 7; matrix products, arithmetic and copies ran while one was open for 2% -> 3% of each run, Pallas kernels for 10% -> 8%
where the time goes in v2:
time: 309 us; the launch traced here: 307 us
  waiting for transfers between devices  156 us (50%)
  starting transfers between devices  70.3 us (23%)
  Pallas kernels  63.7 us (21%)
  local copies, waits for them, and re-layouts  8.68 us (3%)
  other arithmetic  5.96 us (2%)
    all_to_all x6, waiting for transfers between devices, exchange(): return lax.all_to_all(array, axes, split_axis=0, concat_axis=0, tiled=True)  109 us
    all_to_all x6, starting transfers between devices, exchange(): return lax.all_to_all(array, axes, split_axis=0, concat_axis=0, tiled=True)  69.2 us
    ppermute x1, waiting for transfers between devices, layer(): far = lax.ppermute(near, 'blk_1', [(0, 1), (1, 0)])  45.3 us
    pallas_call x1, Pallas kernels, expert(): pl.pallas_call(expert_kernel, in_specs=[pl.BlockSpec(memory_space=pltpu.V...  20.7 us
    pallas_call x1, Pallas kernels, attend(): pl.pallas_call(attend_kernel, grid_spec=pltpu.PrefetchScalarGridSpec(num_...  14.4 us
    pallas_call x1, Pallas kernels, combine(): pl.pallas_call(combine_kernel, in_specs=[pl.BlockSpec(memory_space=pltpu....  9.97 us
    pallas_call x1, Pallas kernels, attend_back(): pl.pallas_call(attend_back_kernel, in_specs=[pl.BlockSpec(memory_space=pl...  9.75 us
    unnamed x19, local copies, waits for them, and re-layouts  6.74 us
  transfers between devices with their start and end apart: 10, of which 7 were waited for; matrix products, arithmetic and copies ran while one was open for 3% of the time, Pallas kernels for 8%

profile of v2, /device:TPU:0, one launch (start us, length us, event | category | flops | bytes accessed | tf_op | source)
XLA Modules:
  0.0 307.3 jit_solution(14833918339584089462)
XLA Ops:
  2.4 5.4 %all-to-all-start = ((bf16[4,128,512]{2,1,0:T(8,128)(2,1)}), bf16[4,128,512]{2,1,0:T(8,128)(2,1)S(1)}, u32[]{:S(2)}, u32[]{:S(2)}) async-start(bf16[4,128,512]{2,1,0:T(8,128)(2,1)} %broadcast_in_dim.42), calls=%async_computation | async-start | bytes 1048576 | tf_op jit(solution)/shard_map/all_to_all | solution.py:745
  9.5 4.3 %place.1 = bf16[384,32,128]{2,1,0:T(8,128)(2,1)} custom-call(s32[256]{0:T(256)} %multiply_add_fusion.slots, bf16[128,4096]{1,0:T(8,128)(2,1)} %bitcast.29), custom_call_target="tpu_custom_call" | custom-call | bytes 4194304 | tf_op jit(solution)/shard_map/place/pallas_call | solution.py:288
  13.7 3.5 %all-to-all-done.near_hbm = bf16[4,128,512]{2,1,0:T(8,128)(2,1)S(1)} async-done(((bf16[4,128,512]{2,1,0:T(8,128)(2,1)}), bf16[4,128,512]{2,1,0:T(8,128)(2,1)S(1)}, u32[]{:S(2)}, u32[]{:S(2)}) %all-to-all-start) | async-done | bytes 524320 | tf_op jit(solution)/shard_map/all_to_all | solution.py:745
  18.1 8.2 %all-to-all-start.2 = ((bf16[128,96,128]{2,1,0:T(8,128)(2,1)}), bf16[128,96,128]{2,1,0:T(8,128)(2,1)S(1)}, u32[]{:S(2)}, u32[]{:S(2)}) async-start(bf16[128,96,128]{2,1,0:T(8,128)(2,1)} %bitcast.28), calls=%async_computation.2 | async-start | bytes 6291456 | tf_op jit(solution)/shard_map/all_to_all | solution.py:745
  26.3 1.0 collective-permute-start
  27.3 45.3 %collective-permute-done.far_hbm = bf16[4,128,512]{2,1,0:T(8,128)(2,1)} collective-permute-done((bf16[4,128,512]{2,1,0:T(8,128)(2,1)}, bf16[4,128,512]{2,1,0:T(8,128)(2,1)}, u32[]{:S(2)}, u32[]{:S(2)}) %collective-permute-start) | collective-permute-done | bytes 524320 | tf_op jit(solution)/shard_map/ppermute | solution.py:765
  73.3 1.6 collective-permute-done.2.far_other_hbm
  74.9 14.4 %attend.1 = (bf16[4,8,256,1024]{3,2,1,0:T(8,128)(2,1)}, f32[32,128]{1,0:T(8,128)}, bf16[128,4096]{1,0:T(8,128)(2,1)}, bf16[128,4096]{1,0:T(8,128)(2,1)}, bf16[12...) custom-call(s32[5]{0:T(128)} %pad_add_fusion.meta, s32[256]{0:T(256)} %multiply_add_fusion.slots, ...), custom_call_target="tpu_custom_call" | custom-call | flops 3221225472 | bytes 25165824 | tf_op jit(solution)/shard_map/attend/pallas_call | solution.py:223
  89.3 25.7 %all-to-all-start.1 = ((bf16[128,96,128]{2,1,0:T(8,128)(2,1)}), bf16[128,96,128]{2,1,0:T(8,128)(2,1)}, u32[]{:S(2)}, u32[]{:S(2)}) async-start(bf16[128,96,128]{2,1,0:T(8,128)(2,1)} %bitcast.31), calls=%async_computation.1 | async-start | bytes 6291456 | tf_op jit(solution)/shard_map/all_to_all | solution.py:745
  115.0 2.8 copy-done
  117.8 4.6 %down.1.inner_grad_ref = f32[384,768]{1,0:T(8,128)S(1)} custom-call(bf16[128,96,128]{2,1,0:T(8,128)(2,1)S(1)} %all-to-all-done.2.rows_ref, bf16[768,4096]{1,0:T(8,128)(2,1)S(1)} %bitcast.23), custom_call_target="tpu_custom_call" | custom-call | flops 2415919104 | bytes 11534336 | tf_op jit(solution)/shard_map/down/pallas_call | solution.py:516
  123.4 32.8 %all-to-all-done.1.rows_ref = bf16[128,96,128]{2,1,0:T(8,128)(2,1)} async-done(((bf16[128,96,128]{2,1,0:T(8,128)(2,1)}), bf16[128,96,128]{2,1,0:T(8,128)(2,1)}, u32[]{:S(2)}, u32[]{:S(2)}) %all-to-all-start.1) | async-done | bytes 3145760 | tf_op jit(solution)/shard_map/all_to_all | solution.py:745
  156.2 1.3 copy-done.3
  157.5 20.7 %expert.1 = bf16[128,104,128]{2,1,0:T(8,128)(2,1)} custom-call(bf16[128,96,128]{2,1,0:T(8,128)(2,1)} %all-to-all-done.1.rows_ref, f32[384,768]{1,0:T(8,128)S(1)} %copy-done.3, bf16[4096,768]{1,0:T(8,128)(2,1)} %bitcast.34, bf16[4096,768]{1,0:T(8,128)(2,1)} %bitcast.35), custom_call_target="tpu_custom_call" | custom-call | flops 9663676416 | bytes 20971520 | tf_op jit(solution)/shard_map/expert/pallas_call | solution.py:612
  178.2 5.9 %all-to-all-start.3 = ((bf16[128,104,128]{2,1,0:T(8,128)(2,1)}), bf16[128,104,128]{2,1,0:T(8,128)(2,1)}, u32[]{:S(2)}, u32[]{:S(2)}) async-start(bf16[128,104,128]{2,1,0:T(8,128)(2,1)} %expert.1), calls=%async_computation.3 | async-start | bytes 6815744 | tf_op jit(solution)/shard_map/all_to_all | solution.py:745
  184.2 1.7 fusion.1
  186.4 41.8 %all-to-all-done.3.back_ref = bf16[128,104,128]{2,1,0:T(8,128)(2,1)} async-done(((bf16[128,104,128]{2,1,0:T(8,128)(2,1)}), bf16[128,104,128]{2,1,0:T(8,128)(2,1)}, u32[]{:S(2)}, u32[]{:S(2)}) %all-to-all-start.3) | async-done | bytes 3407904 | tf_op jit(solution)/shard_map/all_to_all | solution.py:745
  228.2 10.0 %combine.1 = (bf16[128,4096]{1,0:T(8,128)(2,1)}, bf16[4096,128]{1,0:T(8,128)(2,1)}) custom-call(s32[256]{0:T(256)S(1)} %reshape_squeeze.4.ids_smem, s32[256]{0:T(256)S(1)} %convert_reduce_fusion.1.ranks, f32[256]{0:T(256)S(1)} %reshape.27.gates_smem, bf16[128,104,128]{2,1,0:T(8,128)(2,1)} %all-to-all-done.3.back_ref, f32[128,2]{1,0:T(8,128)S(1)} %copy.27.gates_ref, ...), custom_call_target="tpu_custom_call" | custom-call | flops 268435456 | bytes 9437184 | tf_op jit(solution)/shard_map/combine/pallas_call | solution.py:717
  238.2 9.7 %attend_back.1 = (bf16[128,4096]{1,0:T(8,128)(2,1)}, bf16[8,128,512]{2,1,0:T(8,128)(2,1)}, bf16[8,128,512]{2,1,0:T(8,128)(2,1)}) custom-call(s32[5]{0:T(128)} %pad_add_fusion.meta, bf16[128,4096]{1,0:T(8,128)(2,1)} %bitcast.38, bf16[128,4096]{1,0:T(8,128)(2,1)} %get-tuple-element.21.grad_hbm, bf16[128,4096]{1,0:T(8,128)(2,1)} %get-tuple-element.22.att_hbm, ...), custom_call_target="tpu_custom_call" | custom-call | flops 6442450944 | bytes 20971520 | tf_op jit(solution)/shard_map/attend_back/pallas_call | solution.py:445
  248.0 20.5 %all-to-all-start.5 = ((bf16[128,32,128]{2,1,0:T(8,128)(2,1)}), bf16[128,32,128]{2,1,0:T(8,128)(2,1)S(1)}, u32[]{:S(2)}, u32[]{:S(2)}) async-start(bf16[128,32,128]{2,1,0:T(8,128)(2,1)} %bitcast.18), calls=%async_computation.5 | async-start | bytes 2097152 | tf_op jit(solution)/shard_map/all_to_all | solution.py:745
  268.5 2.5 add_convert_fusion
  271.0 16.6 %all-to-all-done.5 = bf16[128,32,128]{2,1,0:T(8,128)(2,1)S(1)} async-done(((bf16[128,32,128]{2,1,0:T(8,128)(2,1)}), bf16[128,32,128]{2,1,0:T(8,128)(2,1)S(1)}, u32[]{:S(2)}, u32[]{:S(2)}) %all-to-all-start.5) | async-done | bytes 1048608 | tf_op jit(solution)/shard_map/all_to_all | solution.py:745
  287.6 3.6 %all-to-all-start.4 = ((bf16[8,128,512]{2,1,0:T(8,128)(2,1)}), bf16[8,128,512]{2,1,0:T(8,128)(2,1)S(1)}, u32[]{:S(2)}, u32[]{:S(2)}) async-start(bf16[8,128,512]{2,1,0:T(8,128)(2,1)} %add_convert_fusion), calls=%async_computation.4 | async-start | bytes 2097152 | tf_op jit(solution)/shard_map/all_to_all | solution.py:745
  292.0 14.5 %all-to-all-done.4 = bf16[8,128,512]{2,1,0:T(8,128)(2,1)S(1)} async-done(((bf16[8,128,512]{2,1,0:T(8,128)(2,1)}), bf16[8,128,512]{2,1,0:T(8,128)(2,1)S(1)}, u32[]{:S(2)}, u32[]{:S(2)}) %all-to-all-start.4) | async-done | bytes 1048608 | tf_op jit(solution)/shard_map/all_to_all | solution.py:745
  (38 shorter events, 8.2 us)
Async XLA Ops:
  2.4 14.9 %all-to-all-start = ((bf16[4,128,512]{2,1,0:T(8,128)(2,1)}), bf16[4,128,512]{2,1,0:T(8,128)(2,1)S(1)}, u32[]{:S(2)}, u32[]{:S(2)}) async-start(bf16[4,128,512]{2,1,0:T(8,128)(2,1)} %broadcast_in_dim.42), calls=%async_computation | async-start | bytes 1048576 | tf_op jit(solution)/shard_map/all_to_all | solution.py:745
  17.2 0.9 copy-start.7
  17.2 55.4 %copy-start.8 = (s32[1,4]{1,0:T(1,128)S(1)}, s32[1,4]{1,0:T(1,128)}, u32[]{:S(2)}) copy-start(s32[1,4]{1,0:T(1,128)} %param.21) | copy-start | bytes 52
  18.1 71.2 %all-to-all-start.2 = ((bf16[128,96,128]{2,1,0:T(8,128)(2,1)}), bf16[128,96,128]{2,1,0:T(8,128)(2,1)S(1)}, u32[]{:S(2)}, u32[]{:S(2)}) async-start(bf16[128,96,128]{2,1,0:T(8,128)(2,1)} %bitcast.28), calls=%async_computation.2 | async-start | bytes 6291456 | tf_op jit(solution)/shard_map/all_to_all | solution.py:745
  26.3 46.3 %collective-permute-start = (bf16[4,128,512]{2,1,0:T(8,128)(2,1)}, bf16[4,128,512]{2,1,0:T(8,128)(2,1)}, u32[]{:S(2)}, u32[]{:S(2)}) collective-permute-start(bf16[4,128,512]{2,1,0:T(8,128)(2,1)} %copy-done.7), channel_id=1, source_target_pairs={{0,2},{2,0},{1,3},{3,1},{4,6},{6,4},{5,7},{7,5},{8,10},{10,8},{9,1... | collective-permute-start | bytes 1572872 | tf_op jit(solution)/shard_map/ppermute | solution.py:765
  27.3 45.9 %collective-permute-start.1 = (bf16[4,128,512]{2,1,0:T(8,128)(2,1)}, bf16[4,128,512]{2,1,0:T(8,128)(2,1)}, u32[]{:S(2)}, u32[]{:S(2)}) collective-permute-start(bf16[4,128,512]{2,1,0:T(8,128)(2,1)} %copy-done.7), channel_id=1, source_target_pairs={{0,1},{1,0},{2,3},{3,2},{4,5},{5,4},{6,7},{7,6},{8,9},{9,8},{10,11... | collective-permute-start | bytes 1572872 | tf_op jit(solution)/shard_map/ppermute | solution.py:741
  72.6 2.3 collective-permute-start.2
  89.3 66.9 %all-to-all-start.1 = ((bf16[128,96,128]{2,1,0:T(8,128)(2,1)}), bf16[128,96,128]{2,1,0:T(8,128)(2,1)}, u32[]{:S(2)}, u32[]{:S(2)}) async-start(bf16[128,96,128]{2,1,0:T(8,128)(2,1)} %bitcast.31), calls=%async_computation.1 | async-start | bytes 6291456 | tf_op jit(solution)/shard_map/all_to_all | solution.py:745
  115.0 2.8 copy-start
  122.4 1.0 copy-start.2
  156.2 1.3 copy-start.3
  178.2 6.0 %copy-start.1 = (bf16[128,4096]{1,0:T(8,128)(2,1)S(1)}, bf16[128,4096]{1,0:T(8,128)(2,1)}, u32[]{:S(2)}) copy-start(bf16[128,4096]{1,0:T(8,128)(2,1)} %get-tuple-element.17.norm_ref) | copy-start | bytes 3145732
  178.2 50.0 %copy-start.4 = (bf16[128,4096]{1,0:T(8,128)(2,1)S(1)}, bf16[128,4096]{1,0:T(8,128)(2,1)}, u32[]{:S(2)}) copy-start(bf16[128,4096]{1,0:T(8,128)(2,1)} %get-tuple-element.19.hid_ref) | copy-start | bytes 3145732
  178.2 50.0 %copy-start.5 = (f32[128,128]{1,0:T(8,128)S(1)}, f32[128,128]{1,0:T(8,128)}, u32[]{:S(2)}) copy-start(f32[128,128]{1,0:T(8,128)} %get-tuple-element.20.rms_ref) | copy-start | bytes 196612
  178.2 50.0 %copy-start.6 = (f32[4096]{0:T(1024)S(1)}, f32[4096]{0:T(1024)}, u32[]{:S(2)}) copy-start(f32[4096]{0:T(1024)} %param.16) | copy-start | bytes 49156
  178.2 50.0 %all-to-all-start.3 = ((bf16[128,104,128]{2,1,0:T(8,128)(2,1)}), bf16[128,104,128]{2,1,0:T(8,128)(2,1)}, u32[]{:S(2)}, u32[]{:S(2)}) async-start(bf16[128,104,128]{2,1,0:T(8,128)(2,1)} %expert.1), calls=%async_computation.3 | async-start | bytes 6815744 | tf_op jit(solution)/shard_map/all_to_all | solution.py:745
  247.9 20.6 %collective-permute-start.3 = (bf16[8,128,512]{2,1,0:T(8,128)(2,1)}, bf16[8,128,512]{2,1,0:T(8,128)(2,1)S(1)}, u32[]{:S(2)}, u32[]{:S(2)}) collective-permute-start(bf16[8,128,512]{2,1,0:T(8,128)(2,1)} %get-tuple-element.27), channel_id=1, source_target_pairs={{0,1},{1,0},{2,3},{3,2},{4,5},{5,4},{6,7},{7,6},{8,9},{9,8},{10,11... | collective-permute-start | bytes 3145736 | tf_op jit(solution)/shard_map/ppermute | solution.py:741
  248.0 39.6 %all-to-all-start.5 = ((bf16[128,32,128]{2,1,0:T(8,128)(2,1)}), bf16[128,32,128]{2,1,0:T(8,128)(2,1)S(1)}, u32[]{:S(2)}, u32[]{:S(2)}) async-start(bf16[128,32,128]{2,1,0:T(8,128)(2,1)} %bitcast.18), calls=%async_computation.5 | async-start | bytes 2097152 | tf_op jit(solution)/shard_map/all_to_all | solution.py:745
  287.6 18.9 %all-to-all-start.4 = ((bf16[8,128,512]{2,1,0:T(8,128)(2,1)}), bf16[8,128,512]{2,1,0:T(8,128)(2,1)S(1)}, u32[]{:S(2)}, u32[]{:S(2)}) async-start(bf16[8,128,512]{2,1,0:T(8,128)(2,1)} %add_convert_fusion), calls=%async_computation.4 | async-start | bytes 2097152 | tf_op jit(solution)/shard_map/all_to_all | solution.py:745

commit v3 on v2

--- a/solution.py
+++ b/solution.py
@@ -367,7 +367,8 @@
     inverse = jnp.concatenate(
         [linv_ref[...], jnp.zeros((128 - QUERY_HEADS, tokens), f32)], axis=0
     ).T
-    ones = jnp.ones((8, HEAD_SIZE), bf16)
+    lane = lax.broadcasted_iota(jnp.int32, (HEAD_SIZE, HEAD_SIZE), 1)
+    dots = jnp.zeros((tokens, HEAD_SIZE), f32)
     for copy in loads:
         copy.wait()
     for h in range(QUERY_HEADS):
@@ -379,7 +380,11 @@
         product = scaled.astype(f32) * att_ref[:, columns].astype(f32)
         head = product.astype(bf16)
         tail = (product - head.astype(f32)).astype(bf16)
-        rd_scr[:, rows] = dot32(ones, head, NT) + dot32(ones, tail, NT)
+        ones = jnp.where(lane == h, 1.0, 0.0).astype(bf16)
+        dots = dots + dot32(head, ones) + dot32(tail, ones)
+    dots = dots.T
+    for h in range(QUERY_HEADS):
+        rd_scr[0:1, h * tokens : (h + 1) * tokens] = dots[h : h + 1, :]
 
     is_first = jnp.full((128, HEAD_SIZE), core, jnp.int32) == 0
 
@@ -474,7 +479,7 @@
     )(meta, queries, grads, attended, linv, *sources, weights)
 
 
-def turn_rows(rows_ref, turn_scr, x_scr):
+def turn_rows(rows_ref, turn_scr, x_scr, between=lambda: None):
     peers, per_peer = rows_ref.shape[0], rows_ref.shape[1]
     capacity = per_peer // QUERY_HEADS
     count = peers * capacity
@@ -485,7 +490,8 @@
             turn_scr[pl.ds((i * capacity + c) * PITCH, QUERY_HEADS), :] = row
         return 0
 
-    lax.fori_loop(0, peers, widen, 0, unroll=2)
+    lax.fori_loop(0, peers, widen, 0, unroll=4)
+    between()
 
     def turn(j, _):
         x_scr[:, lanes(j * HEAD_SIZE, HEAD_SIZE)] = turn_scr[
@@ -561,10 +567,14 @@
             pltpu.make_async_copy(up_hbm.at[:, columns], up_ref.at[:, columns], sems.at[1, n]),
         )
 
-    for n in range(parts):
+    def start(n):
         for copy in load(n):
             copy.start()
-    turn_rows(rows_ref, turn_scr, x_scr)
+
+    start(0)
+    turn_rows(rows_ref, turn_scr, x_scr, lambda: start(1))
+    for n in range(2, parts):
+        start(n)
     score_scr[...] = jnp.zeros_like(score_scr)
 
     def hidden_part(n, _):
@@ -586,13 +596,15 @@
     lax.fori_loop(0, parts, hidden_part, 0)
 
     def grad_part(j, _):
-        rows = pl.ds(pl.multiple_of(j * span, span), span)
+        rows = pl.ds(pl.multiple_of(j * 2 * span, 2 * span), 2 * span)
         d = dot32(da_scr[...], gate_ref[rows, :], NT) + dot32(db_scr[...], up_ref[rows, :], NT)
-        turn_scr[pl.ds(2 * j, count, stride=PITCH), :] = d[:, :HEAD_SIZE]
-        turn_scr[pl.ds(2 * j + 1, count, stride=PITCH), :] = d[:, HEAD_SIZE:]
-        return 0
-
-    lax.fori_loop(0, QUERY_HEADS // 2, grad_part, 0)
+        for i in range(4):
+            turn_scr[pl.ds(4 * j + i, count, stride=PITCH), :] = d[
+                :, i * HEAD_SIZE : (i + 1) * HEAD_SIZE
+            ]
+        return 0
+
+    lax.fori_loop(0, QUERY_HEADS // 4, grad_part, 0)
 
     def narrow(i, _):
         for c in range(capacity):
@@ -737,6 +749,52 @@
     )(ids.reshape(-1), ranks, gates.reshape(-1), back, gates, ids, hidden, normed, inv_rms, out_grad, gain, router)
 
 
+def pair_kernel(keep_ref, came_ref, out_ref):
+    def one(b, _):
+        out_ref[b] = (keep_ref[b].astype(jnp.float32) + came_ref[b].astype(jnp.float32)).astype(
+            jnp.bfloat16
+        )
+        return 0
+
+    lax.fori_loop(0, keep_ref.shape[0], one, 0)
+
+
+def pair_sum(keep, came):
+    vmem = pl.BlockSpec(memory_space=pltpu.VMEM)
+    return pl.pallas_call(
+        pair_kernel,
+        in_specs=[vmem] * 2,
+        out_specs=vmem,
+        out_shape=jax.ShapeDtypeStruct(keep.shape, keep.dtype),
+        compiler_params=pltpu.CompilerParams(vmem_limit_bytes=50 << 20),
+        cost_estimate=pl.CostEstimate(flops=keep.size, bytes_accessed=3 << 20, transcendentals=0),
+        name="pair_sum",
+    )(keep, came)
+
+
+def block_sum_kernel(parts_ref, keys_ref, values_ref):
+    total = parts_ref[0].astype(jnp.float32)
+    for b in range(1, parts_ref.shape[0]):
+        total = total + parts_ref[b].astype(jnp.float32)
+    half = keys_ref.shape[1]
+    keys_ref[...] = total[:, :half].astype(jnp.bfloat16)
+    values_ref[...] = total[:, half:].astype(jnp.bfloat16)
+
+
+def block_sum(parts):
+    vmem = pl.BlockSpec(memory_space=pltpu.VMEM)
+    shape = jax.ShapeDtypeStruct((parts.shape[1], parts.shape[2] // 2), parts.dtype)
+    return pl.pallas_call(
+        block_sum_kernel,
+        in_specs=[vmem],
+        out_specs=[vmem] * 2,
+        out_shape=[shape, shape],
+        compiler_params=pltpu.CompilerParams(vmem_limit_bytes=50 << 20),
+        cost_estimate=pl.CostEstimate(flops=parts.size, bytes_accessed=2 << 20, transcendentals=0),
+        name="block_sum",
+    )(parts)
+
+
 def swap_cores(array):
     return lax.ppermute(array, CORE, [(0, 1), (1, 0)])
 
@@ -760,8 +818,11 @@
     out_grad,
 ):
     token_rows = queries.shape[1]
-    both = jnp.concatenate([keys[0], values[0]], axis=1)
-    near = exchange(jnp.broadcast_to(both[None], (lax.axis_size("blk_0"), *both.shape)), "blk_0")
+    steps = (lax.axis_size("blk_0"), *keys.shape[1:])
+    both = jnp.concatenate(
+        [jnp.broadcast_to(keys, steps), jnp.broadcast_to(values, steps)], axis=2
+    )
+    near = exchange(both, "blk_0")
     far = lax.ppermute(near, "blk_1", [(0, 1), (1, 0)])
     near_other = swap_cores(near)
     sources = (near, far, near_other, swap_cores(far))
@@ -801,14 +862,13 @@
     query_grad, keep, give = attend_back(
         meta, queries[0], residual_gradient, attended, linv, sources, weights
     )
-    pair_sum = (keep.astype(jnp.float32) + swap_cores(give).astype(jnp.float32)).astype(jnp.bfloat16)
-    summed = jnp.sum(exchange(pair_sum, ZX).astype(jnp.float32), axis=0).astype(jnp.bfloat16)
+    pairs = pair_sum(keep, swap_cores(give))
+    key_grad, value_grad = block_sum(exchange(pairs, ZX))
     router_grad = jnp.sum(got_parts.astype(jnp.float32), axis=0)
-    half = KEY_VALUE_HEADS * HEAD_SIZE
     return (
         query_grad[None],
-        summed[None, :, :half],
-        summed[None, :, half:],
+        key_grad[None],
+        value_grad[None],
         residual_gradient[None],
         router_grad,
     )

time: 309 us -> 308 us (level)
    unnamed x19 -> x23, local copies, waits for them, and re-layouts: 6.74 us -> 7.97 us
  transfers between devices with their start and end apart: 10 -> 10, of which waited for: 7 -> 7; matrix products, arithmetic and copies ran while one was open for 3% -> 1% of each run, Pallas kernels for 8% -> 8%
where the time goes in v3:
time: 308 us; the launch traced here: 306 us
  waiting for transfers between devices  158 us (51%)
  starting transfers between devices  70.4 us (23%)
  Pallas kernels  63.6 us (21%)
  local copies, waits for them, and re-layouts  10.1 us (3%)
  other arithmetic  3.21 us (1%)
    all_to_all x6, waiting for transfers between devices, exchange(): return lax.all_to_all(array, axes, split_axis=0, concat_axis=0, tiled=True)  111 us
    all_to_all x6, starting transfers between devices, exchange(): return lax.all_to_all(array, axes, split_axis=0, concat_axis=0, tiled=True)  69.3 us
    ppermute x1, waiting for transfers between devices, layer(): far = lax.ppermute(near, 'blk_1', [(0, 1), (1, 0)])  45.3 us
    pallas_call x1, Pallas kernels, expert(): pl.pallas_call(expert_kernel, in_specs=[pl.BlockSpec(memory_space=pltpu.V...  19.1 us
    pallas_call x1, Pallas kernels, attend(): pl.pallas_call(attend_kernel, grid_spec=pltpu.PrefetchScalarGridSpec(num_...  14.4 us
    pallas_call x1, Pallas kernels, combine(): pl.pallas_call(combine_kernel, in_specs=[pl.BlockSpec(memory_space=pltpu....  9.97 us
    pallas_call x1, Pallas kernels, attend_back(): pl.pallas_call(attend_back_kernel, in_specs=[pl.BlockSpec(memory_space=pl...  9.43 us
    unnamed x23, local copies, waits for them, and re-layouts  7.97 us
  transfers between devices with their start and end apart: 10, of which 7 were waited for; matrix products, arithmetic and copies ran while one was open for 1% of the time, Pallas kernels for 8%

profile of v3, /device:TPU:0, one launch (start us, length us, event | category | flops | bytes accessed | tf_op | source)
XLA Modules:
  0.0 306.3 jit_solution(12170836677926091586)
XLA Ops:
  3.2 5.4 %all-to-all-start = ((bf16[4,128,512]{2,1,0:T(8,128)(2,1)}), bf16[4,128,512]{2,1,0:T(8,128)(2,1)S(1)}, u32[]{:S(2)}, u32[]{:S(2)}) async-start(bf16[4,128,512]{2,1,0:T(8,128)(2,1)} %pad_maximum_fusion), calls=%async_computation | async-start | bytes 1048576 | tf_op jit(solution)/shard_map/all_to_all | solution.py:803
  10.3 4.2 %place.1 = bf16[384,32,128]{2,1,0:T(8,128)(2,1)} custom-call(s32[256]{0:T(256)} %multiply_add_fusion.slots, bf16[128,4096]{1,0:T(8,128)(2,1)} %bitcast.27), custom_call_target="tpu_custom_call" | custom-call | bytes 4194304 | tf_op jit(solution)/shard_map/place/pallas_call | solution.py:288
  14.5 3.5 %all-to-all-done.near_hbm = bf16[4,128,512]{2,1,0:T(8,128)(2,1)S(1)} async-done(((bf16[4,128,512]{2,1,0:T(8,128)(2,1)}), bf16[4,128,512]{2,1,0:T(8,128)(2,1)S(1)}, u32[]{:S(2)}, u32[]{:S(2)}) %all-to-all-start) | async-done | bytes 524320 | tf_op jit(solution)/shard_map/all_to_all | solution.py:803
  19.0 8.2 %all-to-all-start.2 = ((bf16[128,96,128]{2,1,0:T(8,128)(2,1)}), bf16[128,96,128]{2,1,0:T(8,128)(2,1)S(1)}, u32[]{:S(2)}, u32[]{:S(2)}) async-start(bf16[128,96,128]{2,1,0:T(8,128)(2,1)} %bitcast.26), calls=%async_computation.2 | async-start | bytes 6291456 | tf_op jit(solution)/shard_map/all_to_all | solution.py:803
  27.2 1.0 collective-permute-start
  28.2 45.3 %collective-permute-done.far_hbm = bf16[4,128,512]{2,1,0:T(8,128)(2,1)} collective-permute-done((bf16[4,128,512]{2,1,0:T(8,128)(2,1)}, bf16[4,128,512]{2,1,0:T(8,128)(2,1)}, u32[]{:S(2)}, u32[]{:S(2)}) %collective-permute-start) | collective-permute-done | bytes 524320 | tf_op jit(solution)/shard_map/ppermute | solution.py:826
  74.1 1.6 collective-permute-done.2.far_other_hbm
  75.7 14.4 %attend.1 = (bf16[4,8,256,1024]{3,2,1,0:T(8,128)(2,1)}, f32[32,128]{1,0:T(8,128)}, bf16[128,4096]{1,0:T(8,128)(2,1)}, bf16[128,4096]{1,0:T(8,128)(2,1)}, bf16[12...) custom-call(s32[5]{0:T(128)} %pad_add_fusion.meta, s32[256]{0:T(256)} %multiply_add_fusion.slots, ...), custom_call_target="tpu_custom_call" | custom-call | flops 3221225472 | bytes 25165824 | tf_op jit(solution)/shard_map/attend/pallas_call | solution.py:223
  90.1 25.7 %all-to-all-start.1 = ((bf16[128,96,128]{2,1,0:T(8,128)(2,1)}), bf16[128,96,128]{2,1,0:T(8,128)(2,1)}, u32[]{:S(2)}, u32[]{:S(2)}) async-start(bf16[128,96,128]{2,1,0:T(8,128)(2,1)} %bitcast.29), calls=%async_computation.1 | async-start | bytes 6291456 | tf_op jit(solution)/shard_map/all_to_all | solution.py:803
  115.8 2.8 copy-done
  118.6 4.5 %down.1.inner_grad_ref = f32[384,768]{1,0:T(8,128)S(1)} custom-call(bf16[128,96,128]{2,1,0:T(8,128)(2,1)S(1)} %all-to-all-done.2.rows_ref, bf16[768,4096]{1,0:T(8,128)(2,1)S(1)} %bitcast.21), custom_call_target="tpu_custom_call" | custom-call | flops 2415919104 | bytes 11534336 | tf_op jit(solution)/shard_map/down/pallas_call | solution.py:522
  124.1 32.9 %all-to-all-done.1.rows_ref = bf16[128,96,128]{2,1,0:T(8,128)(2,1)} async-done(((bf16[128,96,128]{2,1,0:T(8,128)(2,1)}), bf16[128,96,128]{2,1,0:T(8,128)(2,1)}, u32[]{:S(2)}, u32[]{:S(2)}) %all-to-all-start.1) | async-done | bytes 3145760 | tf_op jit(solution)/shard_map/all_to_all | solution.py:803
  157.0 1.3 copy-done.3
  158.3 19.1 %expert.1 = bf16[128,104,128]{2,1,0:T(8,128)(2,1)} custom-call(bf16[128,96,128]{2,1,0:T(8,128)(2,1)} %all-to-all-done.1.rows_ref, f32[384,768]{1,0:T(8,128)S(1)} %copy-done.3, bf16[4096,768]{1,0:T(8,128)(2,1)} %bitcast.32, bf16[4096,768]{1,0:T(8,128)(2,1)} %bitcast.33), custom_call_target="tpu_custom_call" | custom-call | flops 9663676416 | bytes 20971520 | tf_op jit(solution)/shard_map/expert/pallas_call | solution.py:624
  177.4 6.0 %all-to-all-start.3 = ((bf16[128,104,128]{2,1,0:T(8,128)(2,1)}), bf16[128,104,128]{2,1,0:T(8,128)(2,1)}, u32[]{:S(2)}, u32[]{:S(2)}) async-start(bf16[128,104,128]{2,1,0:T(8,128)(2,1)} %expert.1), calls=%async_computation.3 | async-start | bytes 6815744 | tf_op jit(solution)/shard_map/all_to_all | solution.py:803
  184.5 43.0 %all-to-all-done.3.back_ref = bf16[128,104,128]{2,1,0:T(8,128)(2,1)} async-done(((bf16[128,104,128]{2,1,0:T(8,128)(2,1)}), bf16[128,104,128]{2,1,0:T(8,128)(2,1)}, u32[]{:S(2)}, u32[]{:S(2)}) %all-to-all-start.3) | async-done | bytes 3407904 | tf_op jit(solution)/shard_map/all_to_all | solution.py:803
  227.5 10.0 %combine.1 = (bf16[128,4096]{1,0:T(8,128)(2,1)}, bf16[4096,128]{1,0:T(8,128)(2,1)}) custom-call(s32[256]{0:T(256)S(1)} %reshape_squeeze.4.ids_smem, s32[256]{0:T(256)S(1)} %convert_reduce_fusion.1.ranks, f32[256]{0:T(256)S(1)} %reshape.26.gates_smem, bf16[128,104,128]{2,1,0:T(8,128)(2,1)} %all-to-all-done.3.back_ref, f32[128,2]{1,0:T(8,128)S(1)} %copy.27.gates_ref, ...), custom_call_target="tpu_custom_call" | custom-call | flops 268435456 | bytes 9437184 | tf_op jit(solution)/shard_map/combine/pallas_call | solution.py:729
  237.5 9.4 %attend_back.1 = (bf16[128,4096]{1,0:T(8,128)(2,1)}, bf16[8,128,512]{2,1,0:T(8,128)(2,1)}, bf16[8,128,512]{2,1,0:T(8,128)(2,1)}) custom-call(s32[5]{0:T(128)} %pad_add_fusion.meta, bf16[128,4096]{1,0:T(8,128)(2,1)} %bitcast.36, bf16[128,4096]{1,0:T(8,128)(2,1)} %get-tuple-element.23.grad_hbm, bf16[128,4096]{1,0:T(8,128)(2,1)} %get-tuple-element.24.att_hbm, ...), custom_call_target="tpu_custom_call" | custom-call | flops 6442450944 | bytes 20971520 | tf_op jit(solution)/shard_map/attend_back/pallas_call | solution.py:450
  247.0 20.5 %all-to-all-start.5 = ((bf16[128,32,128]{2,1,0:T(8,128)(2,1)}), bf16[128,32,128]{2,1,0:T(8,128)(2,1)S(1)}, u32[]{:S(2)}, u32[]{:S(2)}) async-start(bf16[128,32,128]{2,1,0:T(8,128)(2,1)} %bitcast.18), calls=%async_computation.5 | async-start | bytes 2097152 | tf_op jit(solution)/shard_map/all_to_all | solution.py:803
  267.5 1.2 copy-done.5
  268.7 1.3 pair_sum.1
  270.0 16.7 %all-to-all-done.5 = bf16[128,32,128]{2,1,0:T(8,128)(2,1)S(1)} async-done(((bf16[128,32,128]{2,1,0:T(8,128)(2,1)}), bf16[128,32,128]{2,1,0:T(8,128)(2,1)S(1)}, u32[]{:S(2)}, u32[]{:S(2)}) %all-to-all-start.5) | async-done | bytes 1048608 | tf_op jit(solution)/shard_map/all_to_all | solution.py:803
  286.6 3.6 %all-to-all-start.4 = ((bf16[8,128,512]{2,1,0:T(8,128)(2,1)}), bf16[8,128,512]{2,1,0:T(8,128)(2,1)S(1)}, u32[]{:S(2)}, u32[]{:S(2)}) async-start(bf16[8,128,512]{2,1,0:T(8,128)(2,1)} %pair_sum.1), calls=%async_computation.4 | async-start | bytes 2097152 | tf_op jit(solution)/shard_map/all_to_all | solution.py:803
  291.0 14.5 %all-to-all-done.4.parts_ref = bf16[8,128,512]{2,1,0:T(8,128)(2,1)S(1)} async-done(((bf16[8,128,512]{2,1,0:T(8,128)(2,1)}), bf16[8,128,512]{2,1,0:T(8,128)(2,1)S(1)}, u32[]{:S(2)}, u32[]{:S(2)}) %all-to-all-start.4) | async-done | bytes 1048608 | tf_op jit(solution)/shard_map/all_to_all | solution.py:803
  (42 shorter events, 9.4 us)
Async XLA Ops:
  3.2 14.9 %all-to-all-start = ((bf16[4,128,512]{2,1,0:T(8,128)(2,1)}), bf16[4,128,512]{2,1,0:T(8,128)(2,1)S(1)}, u32[]{:S(2)}, u32[]{:S(2)}) async-start(bf16[4,128,512]{2,1,0:T(8,128)(2,1)} %pad_maximum_fusion), calls=%async_computation | async-start | bytes 1048576 | tf_op jit(solution)/shard_map/all_to_all | solution.py:803
  14.5 58.9 %copy-start.10 = (s32[1,4]{1,0:T(1,128)S(1)}, s32[1,4]{1,0:T(1,128)}, u32[]{:S(2)}) copy-start(s32[1,4]{1,0:T(1,128)} %param.21) | copy-start | bytes 52
  18.1 0.9 copy-start.9
  19.0 71.2 %all-to-all-start.2 = ((bf16[128,96,128]{2,1,0:T(8,128)(2,1)}), bf16[128,96,128]{2,1,0:T(8,128)(2,1)S(1)}, u32[]{:S(2)}, u32[]{:S(2)}) async-start(bf16[128,96,128]{2,1,0:T(8,128)(2,1)} %bitcast.26), calls=%async_computation.2 | async-start | bytes 6291456 | tf_op jit(solution)/shard_map/all_to_all | solution.py:803
  27.2 46.3 %collective-permute-start = (bf16[4,128,512]{2,1,0:T(8,128)(2,1)}, bf16[4,128,512]{2,1,0:T(8,128)(2,1)}, u32[]{:S(2)}, u32[]{:S(2)}) collective-permute-start(bf16[4,128,512]{2,1,0:T(8,128)(2,1)} %copy-done.9), channel_id=1, source_target_pairs={{0,2},{2,0},{1,3},{3,1},{4,6},{6,4},{5,7},{7,5},{8,10},{10,8},{9,1... | collective-permute-start | bytes 1572872 | tf_op jit(solution)/shard_map/ppermute | solution.py:826
  28.2 45.9 %collective-permute-start.1 = (bf16[4,128,512]{2,1,0:T(8,128)(2,1)}, bf16[4,128,512]{2,1,0:T(8,128)(2,1)}, u32[]{:S(2)}, u32[]{:S(2)}) collective-permute-start(bf16[4,128,512]{2,1,0:T(8,128)(2,1)} %copy-done.9), channel_id=1, source_target_pairs={{0,1},{1,0},{2,3},{3,2},{4,5},{5,4},{6,7},{7,6},{8,9},{9,8},{10,11... | collective-permute-start | bytes 1572872 | tf_op jit(solution)/shard_map/ppermute | solution.py:799
  73.5 2.3 collective-permute-start.2
  90.1 66.9 %all-to-all-start.1 = ((bf16[128,96,128]{2,1,0:T(8,128)(2,1)}), bf16[128,96,128]{2,1,0:T(8,128)(2,1)}, u32[]{:S(2)}, u32[]{:S(2)}) async-start(bf16[128,96,128]{2,1,0:T(8,128)(2,1)} %bitcast.29), calls=%async_computation.1 | async-start | bytes 6291456 | tf_op jit(solution)/shard_map/all_to_all | solution.py:803
  115.8 2.8 copy-start
  123.1 1.0 copy-start.2
  157.0 1.3 copy-start.3
  177.4 6.2 %copy-start.1 = (bf16[128,4096]{1,0:T(8,128)(2,1)S(1)}, bf16[128,4096]{1,0:T(8,128)(2,1)}, u32[]{:S(2)}) copy-start(bf16[128,4096]{1,0:T(8,128)(2,1)} %get-tuple-element.19.norm_ref) | copy-start | bytes 3145732
  177.4 6.2 %copy-start.8 = (bf16[4096,128]{1,0:T(8,128)(2,1)S(1)}, bf16[4096,128]{1,0:T(8,128)(2,1)}, u32[]{:S(2)}) copy-start(bf16[4096,128]{1,0:T(8,128)(2,1)} %router_ref.1) | copy-start | bytes 3145732
  177.4 50.1 %copy-start.4 = (bf16[128,4096]{1,0:T(8,128)(2,1)S(1)}, bf16[128,4096]{1,0:T(8,128)(2,1)}, u32[]{:S(2)}) copy-start(bf16[128,4096]{1,0:T(8,128)(2,1)} %get-tuple-element.21.hid_ref) | copy-start | bytes 3145732
  177.4 50.1 %copy-start.6 = (f32[128,128]{1,0:T(8,128)S(1)}, f32[128,128]{1,0:T(8,128)}, u32[]{:S(2)}) copy-start(f32[128,128]{1,0:T(8,128)} %get-tuple-element.22.rms_ref) | copy-start | bytes 196612
  177.4 50.1 %copy-start.7 = (f32[4096]{0:T(1024)S(1)}, f32[4096]{0:T(1024)}, u32[]{:S(2)}) copy-start(f32[4096]{0:T(1024)} %param.16) | copy-start | bytes 49156
  177.4 50.1 %all-to-all-start.3 = ((bf16[128,104,128]{2,1,0:T(8,128)(2,1)}), bf16[128,104,128]{2,1,0:T(8,128)(2,1)}, u32[]{:S(2)}, u32[]{:S(2)}) async-start(bf16[128,104,128]{2,1,0:T(8,128)(2,1)} %expert.1), calls=%async_computation.3 | async-start | bytes 6815744 | tf_op jit(solution)/shard_map/all_to_all | solution.py:803
  246.9 20.6 %collective-permute-start.3 = (bf16[8,128,512]{2,1,0:T(8,128)(2,1)}, bf16[8,128,512]{2,1,0:T(8,128)(2,1)S(1)}, u32[]{:S(2)}, u32[]{:S(2)}) collective-permute-start(bf16[8,128,512]{2,1,0:T(8,128)(2,1)} %get-tuple-element.29), channel_id=1, source_target_pairs={{0,1},{1,0},{2,3},{3,2},{4,5},{5,4},{6,7},{7,6},{8,9},{9,8},{10,11... | collective-permute-start | bytes 3145736 | tf_op jit(solution)/shard_map/ppermute | solution.py:799
  247.0 39.6 %all-to-all-start.5 = ((bf16[128,32,128]{2,1,0:T(8,128)(2,1)}), bf16[128,32,128]{2,1,0:T(8,128)(2,1)S(1)}, u32[]{:S(2)}, u32[]{:S(2)}) async-start(bf16[128,32,128]{2,1,0:T(8,128)(2,1)} %bitcast.18), calls=%async_computation.5 | async-start | bytes 2097152 | tf_op jit(solution)/shard_map/all_to_all | solution.py:803
  267.5 1.2 copy-start.5
  286.6 18.9 %all-to-all-start.4 = ((bf16[8,128,512]{2,1,0:T(8,128)(2,1)}), bf16[8,128,512]{2,1,0:T(8,128)(2,1)S(1)}, u32[]{:S(2)}, u32[]{:S(2)}) async-start(bf16[8,128,512]{2,1,0:T(8,128)(2,1)} %pair_sum.1), calls=%async_computation.4 | async-start | bytes 2097152 | tf_op jit(solution)/shard_map/all_to_all | solution.py:803

commit v4 on v3

--- a/solution.py
+++ b/solution.py
@@ -637,7 +637,7 @@
             pltpu.SemaphoreType.DMA((2, hidden_units // 256)),
         ],
         out_shape=jax.ShapeDtypeStruct((peers, per_peer + 8, HEAD_SIZE), bf16),
-        compiler_params=pltpu.CompilerParams(vmem_limit_bytes=50 << 20),
+        compiler_params=pltpu.CompilerParams(vmem_limit_bytes=53 << 20),
         cost_estimate=pl.CostEstimate(
             flops=8 * count * width * hidden_units, bytes_accessed=20 << 20, transcendentals=count * hidden_units
         ),
@@ -766,7 +766,7 @@
         in_specs=[vmem] * 2,
         out_specs=vmem,
         out_shape=jax.ShapeDtypeStruct(keep.shape, keep.dtype),
-        compiler_params=pltpu.CompilerParams(vmem_limit_bytes=50 << 20),
+        compiler_params=pltpu.CompilerParams(vmem_limit_bytes=59 << 20),
         cost_estimate=pl.CostEstimate(flops=keep.size, bytes_accessed=3 << 20, transcendentals=0),
         name="pair_sum",
     )(keep, came)
@@ -818,11 +818,8 @@
     out_grad,
 ):
     token_rows = queries.shape[1]
-    steps = (lax.axis_size("blk_0"), *keys.shape[1:])
-    both = jnp.concatenate(
-        [jnp.broadcast_to(keys, steps), jnp.broadcast_to(values, steps)], axis=2
-    )
-    near = exchange(both, "blk_0")
+    both = jnp.concatenate([keys[0], values[0]], axis=1)
+    near = exchange(jnp.broadcast_to(both[None], (lax.axis_size("blk_0"), *both.shape)), "blk_0")
     far = lax.ppermute(near, "blk_1", [(0, 1), (1, 0)])
     near_other = swap_cores(near)
     sources = (near, far, near_other, swap_cores(far))

time: 308 us -> 306 us (level)
    unnamed x23 -> x21, local copies, waits for them, and re-layouts: 7.97 us -> 6.41 us
  transfers between devices with their start and end apart: 10 -> 10, of which waited for: 7 -> 7; matrix products, arithmetic and copies ran while one was open for 1% -> 1% of each run, Pallas kernels for 8% -> 9%
where the time goes in v4:
time: 306 us; the launch traced here: 304 us
  waiting for transfers between devices  156 us (51%)
  starting transfers between devices  70.5 us (23%)
  Pallas kernels  65.5 us (21%)
  local copies, waits for them, and re-layouts  7.69 us (3%)
  other arithmetic  3.29 us (1%)
    all_to_all x6, waiting for transfers between devices, exchange(): return lax.all_to_all(array, axes, split_axis=0, concat_axis=0, tiled=True)  109 us
    all_to_all x6, starting transfers between devices, exchange(): return lax.all_to_all(array, axes, split_axis=0, concat_axis=0, tiled=True)  69.3 us
    ppermute x1, waiting for transfers between devices, layer(): far = lax.ppermute(near, 'blk_1', [(0, 1), (1, 0)])  45.3 us
    pallas_call x1, Pallas kernels, expert(): pl.pallas_call(expert_kernel, in_specs=[pl.BlockSpec(memory_space=pltpu.V...  19.4 us
    pallas_call x1, Pallas kernels, attend(): pl.pallas_call(attend_kernel, grid_spec=pltpu.PrefetchScalarGridSpec(num_...  14.4 us
    pallas_call x1, Pallas kernels, combine(): pl.pallas_call(combine_kernel, in_specs=[pl.BlockSpec(memory_space=pltpu....  9.97 us
    pallas_call x1, Pallas kernels, attend_back(): pl.pallas_call(attend_back_kernel, in_specs=[pl.BlockSpec(memory_space=pl...  9.41 us
    unnamed x21, local copies, waits for them, and re-layouts  6.41 us
  transfers between devices with their start and end apart: 10, of which 7 were waited for; matrix products, arithmetic and copies ran while one was open for 1% of the time, Pallas kernels for 9%

profile of v4, /device:TPU:0, one launch (start us, length us, event | category | flops | bytes accessed | tf_op | source)
XLA Modules:
  0.0 304.4 jit_solution(16685439893640317740)
XLA Ops:
  2.4 5.4 %all-to-all-start = ((bf16[4,128,512]{2,1,0:T(8,128)(2,1)}), bf16[4,128,512]{2,1,0:T(8,128)(2,1)S(1)}, u32[]{:S(2)}, u32[]{:S(2)}) async-start(bf16[4,128,512]{2,1,0:T(8,128)(2,1)} %broadcast_in_dim.42), calls=%async_computation | async-start | bytes 1048576 | tf_op jit(solution)/shard_map/all_to_all | solution.py:803
  9.5 4.2 %place.1 = bf16[384,32,128]{2,1,0:T(8,128)(2,1)} custom-call(s32[256]{0:T(256)} %multiply_add_fusion.slots, bf16[128,4096]{1,0:T(8,128)(2,1)} %bitcast.27), custom_call_target="tpu_custom_call" | custom-call | bytes 4194304 | tf_op jit(solution)/shard_map/place/pallas_call | solution.py:288
  13.7 3.5 %all-to-all-done.near_hbm = bf16[4,128,512]{2,1,0:T(8,128)(2,1)S(1)} async-done(((bf16[4,128,512]{2,1,0:T(8,128)(2,1)}), bf16[4,128,512]{2,1,0:T(8,128)(2,1)S(1)}, u32[]{:S(2)}, u32[]{:S(2)}) %all-to-all-start) | async-done | bytes 524320 | tf_op jit(solution)/shard_map/all_to_all | solution.py:803
  18.1 8.2 %all-to-all-start.2 = ((bf16[128,96,128]{2,1,0:T(8,128)(2,1)}), bf16[128,96,128]{2,1,0:T(8,128)(2,1)S(1)}, u32[]{:S(2)}, u32[]{:S(2)}) async-start(bf16[128,96,128]{2,1,0:T(8,128)(2,1)} %bitcast.26), calls=%async_computation.2 | async-start | bytes 6291456 | tf_op jit(solution)/shard_map/all_to_all | solution.py:803
  26.3 1.0 collective-permute-start
  27.3 45.3 %collective-permute-done.far_hbm = bf16[4,128,512]{2,1,0:T(8,128)(2,1)} collective-permute-done((bf16[4,128,512]{2,1,0:T(8,128)(2,1)}, bf16[4,128,512]{2,1,0:T(8,128)(2,1)}, u32[]{:S(2)}, u32[]{:S(2)}) %collective-permute-start) | collective-permute-done | bytes 524320 | tf_op jit(solution)/shard_map/ppermute | solution.py:823
  73.2 1.6 collective-permute-done.2.far_other_hbm
  74.8 14.4 %attend.1 = (bf16[4,8,256,1024]{3,2,1,0:T(8,128)(2,1)}, f32[32,128]{1,0:T(8,128)}, bf16[128,4096]{1,0:T(8,128)(2,1)}, bf16[128,4096]{1,0:T(8,128)(2,1)}, bf16[12...) custom-call(s32[5]{0:T(128)} %pad_add_fusion.meta, s32[256]{0:T(256)} %multiply_add_fusion.slots, ...), custom_call_target="tpu_custom_call" | custom-call | flops 3221225472 | bytes 25165824 | tf_op jit(solution)/shard_map/attend/pallas_call | solution.py:223
  89.2 25.7 %all-to-all-start.1 = ((bf16[128,96,128]{2,1,0:T(8,128)(2,1)}), bf16[128,96,128]{2,1,0:T(8,128)(2,1)}, u32[]{:S(2)}, u32[]{:S(2)}) async-start(bf16[128,96,128]{2,1,0:T(8,128)(2,1)} %bitcast.29), calls=%async_computation.1 | async-start | bytes 6291456 | tf_op jit(solution)/shard_map/all_to_all | solution.py:803
  114.9 2.8 copy-done
  117.7 4.5 %down.1.inner_grad_ref = f32[384,768]{1,0:T(8,128)S(1)} custom-call(bf16[128,96,128]{2,1,0:T(8,128)(2,1)S(1)} %all-to-all-done.2.rows_ref, bf16[768,4096]{1,0:T(8,128)(2,1)S(1)} %bitcast.21), custom_call_target="tpu_custom_call" | custom-call | flops 2415919104 | bytes 11534336 | tf_op jit(solution)/shard_map/down/pallas_call | solution.py:522
  122.2 1.0 copy-done.2
  123.2 32.9 %all-to-all-done.1.rows_ref = bf16[128,96,128]{2,1,0:T(8,128)(2,1)} async-done(((bf16[128,96,128]{2,1,0:T(8,128)(2,1)}), bf16[128,96,128]{2,1,0:T(8,128)(2,1)}, u32[]{:S(2)}, u32[]{:S(2)}) %all-to-all-start.1) | async-done | bytes 3145760 | tf_op jit(solution)/shard_map/all_to_all | solution.py:803
  156.1 19.4 %expert.1 = bf16[128,104,128]{2,1,0:T(8,128)(2,1)} custom-call(bf16[128,96,128]{2,1,0:T(8,128)(2,1)} %all-to-all-done.1.rows_ref, f32[384,768]{1,0:T(8,128)} %copy-done.2, bf16[4096,768]{1,0:T(8,128)(2,1)} %bitcast.32, bf16[4096,768]{1,0:T(8,128)(2,1)} %bitcast.33), custom_call_target="tpu_custom_call" | custom-call | flops 9663676416 | bytes 20971520 | tf_op jit(solution)/shard_map/expert/pallas_call | solution.py:624
  175.6 6.0 %all-to-all-start.3 = ((bf16[128,104,128]{2,1,0:T(8,128)(2,1)}), bf16[128,104,128]{2,1,0:T(8,128)(2,1)}, u32[]{:S(2)}, u32[]{:S(2)}) async-start(bf16[128,104,128]{2,1,0:T(8,128)(2,1)} %expert.1), calls=%async_computation.3 | async-start | bytes 6815744 | tf_op jit(solution)/shard_map/all_to_all | solution.py:803
  182.6 43.0 %all-to-all-done.3.back_ref = bf16[128,104,128]{2,1,0:T(8,128)(2,1)} async-done(((bf16[128,104,128]{2,1,0:T(8,128)(2,1)}), bf16[128,104,128]{2,1,0:T(8,128)(2,1)}, u32[]{:S(2)}, u32[]{:S(2)}) %all-to-all-start.3) | async-done | bytes 3407904 | tf_op jit(solution)/shard_map/all_to_all | solution.py:803
  225.7 10.0 %combine.1 = (bf16[128,4096]{1,0:T(8,128)(2,1)}, bf16[4096,128]{1,0:T(8,128)(2,1)}) custom-call(s32[256]{0:T(256)S(1)} %reshape_squeeze.4.ids_smem, s32[256]{0:T(256)S(1)} %convert_reduce_fusion.1.ranks, f32[256]{0:T(256)S(1)} %reshape.27.gates_smem, bf16[128,104,128]{2,1,0:T(8,128)(2,1)} %all-to-all-done.3.back_ref, f32[128,2]{1,0:T(8,128)S(1)} %copy.27.gates_ref, ...), custom_call_target="tpu_custom_call" | custom-call | flops 268435456 | bytes 9437184 | tf_op jit(solution)/shard_map/combine/pallas_call | solution.py:729
  235.6 9.4 %attend_back.1 = (bf16[128,4096]{1,0:T(8,128)(2,1)}, bf16[8,128,512]{2,1,0:T(8,128)(2,1)}, bf16[8,128,512]{2,1,0:T(8,128)(2,1)}) custom-call(s32[5]{0:T(128)} %pad_add_fusion.meta, bf16[128,4096]{1,0:T(8,128)(2,1)} %bitcast.36, bf16[128,4096]{1,0:T(8,128)(2,1)} %get-tuple-element.23.grad_hbm, bf16[128,4096]{1,0:T(8,128)(2,1)} %get-tuple-element.24.att_hbm, ...), custom_call_target="tpu_custom_call" | custom-call | flops 6442450944 | bytes 20971520 | tf_op jit(solution)/shard_map/attend_back/pallas_call | solution.py:450
  245.2 20.5 %all-to-all-start.5 = ((bf16[128,32,128]{2,1,0:T(8,128)(2,1)}), bf16[128,32,128]{2,1,0:T(8,128)(2,1)S(1)}, u32[]{:S(2)}, u32[]{:S(2)}) async-start(bf16[128,32,128]{2,1,0:T(8,128)(2,1)} %bitcast.18), calls=%async_computation.5 | async-start | bytes 2097152 | tf_op jit(solution)/shard_map/all_to_all | solution.py:803
  265.6 1.0 copy-done.7
  266.6 2.8 pair_sum.1
  269.4 15.4 %all-to-all-done.5 = bf16[128,32,128]{2,1,0:T(8,128)(2,1)S(1)} async-done(((bf16[128,32,128]{2,1,0:T(8,128)(2,1)}), bf16[128,32,128]{2,1,0:T(8,128)(2,1)S(1)}, u32[]{:S(2)}, u32[]{:S(2)}) %all-to-all-start.5) | async-done | bytes 1048608 | tf_op jit(solution)/shard_map/all_to_all | solution.py:803
  284.8 3.6 %all-to-all-start.4 = ((bf16[8,128,512]{2,1,0:T(8,128)(2,1)}), bf16[8,128,512]{2,1,0:T(8,128)(2,1)S(1)}, u32[]{:S(2)}, u32[]{:S(2)}) async-start(bf16[8,128,512]{2,1,0:T(8,128)(2,1)} %pair_sum.1), calls=%async_computation.4 | async-start | bytes 2097152 | tf_op jit(solution)/shard_map/all_to_all | solution.py:803
  289.1 14.5 %all-to-all-done.4.parts_ref = bf16[8,128,512]{2,1,0:T(8,128)(2,1)S(1)} async-done(((bf16[8,128,512]{2,1,0:T(8,128)(2,1)}), bf16[8,128,512]{2,1,0:T(8,128)(2,1)S(1)}, u32[]{:S(2)}, u32[]{:S(2)}) %all-to-all-start.4) | async-done | bytes 1048608 | tf_op jit(solution)/shard_map/all_to_all | solution.py:803
  (39 shorter events, 7.5 us)
Async XLA Ops:
  2.4 14.9 %all-to-all-start = ((bf16[4,128,512]{2,1,0:T(8,128)(2,1)}), bf16[4,128,512]{2,1,0:T(8,128)(2,1)S(1)}, u32[]{:S(2)}, u32[]{:S(2)}) async-start(bf16[4,128,512]{2,1,0:T(8,128)(2,1)} %broadcast_in_dim.42), calls=%async_computation | async-start | bytes 1048576 | tf_op jit(solution)/shard_map/all_to_all | solution.py:803
  13.7 58.9 %copy-start.9 = (s32[1,4]{1,0:T(1,128)S(1)}, s32[1,4]{1,0:T(1,128)}, u32[]{:S(2)}) copy-start(s32[1,4]{1,0:T(1,128)} %param.21) | copy-start | bytes 52
  17.2 0.8 copy-start.8
  18.1 71.2 %all-to-all-start.2 = ((bf16[128,96,128]{2,1,0:T(8,128)(2,1)}), bf16[128,96,128]{2,1,0:T(8,128)(2,1)S(1)}, u32[]{:S(2)}, u32[]{:S(2)}) async-start(bf16[128,96,128]{2,1,0:T(8,128)(2,1)} %bitcast.26), calls=%async_computation.2 | async-start | bytes 6291456 | tf_op jit(solution)/shard_map/all_to_all | solution.py:803
  26.3 46.3 %collective-permute-start = (bf16[4,128,512]{2,1,0:T(8,128)(2,1)}, bf16[4,128,512]{2,1,0:T(8,128)(2,1)}, u32[]{:S(2)}, u32[]{:S(2)}) collective-permute-start(bf16[4,128,512]{2,1,0:T(8,128)(2,1)} %copy-done.8), channel_id=1, source_target_pairs={{0,2},{2,0},{1,3},{3,1},{4,6},{6,4},{5,7},{7,5},{8,10},{10,8},{9,1... | collective-permute-start | bytes 1572872 | tf_op jit(solution)/shard_map/ppermute | solution.py:823
  27.3 45.9 %collective-permute-start.1 = (bf16[4,128,512]{2,1,0:T(8,128)(2,1)}, bf16[4,128,512]{2,1,0:T(8,128)(2,1)}, u32[]{:S(2)}, u32[]{:S(2)}) collective-permute-start(bf16[4,128,512]{2,1,0:T(8,128)(2,1)} %copy-done.8), channel_id=1, source_target_pairs={{0,1},{1,0},{2,3},{3,2},{4,5},{5,4},{6,7},{7,6},{8,9},{9,8},{10,11... | collective-permute-start | bytes 1572872 | tf_op jit(solution)/shard_map/ppermute | solution.py:799
  72.6 2.3 collective-permute-start.2
  89.2 66.9 %all-to-all-start.1 = ((bf16[128,96,128]{2,1,0:T(8,128)(2,1)}), bf16[128,96,128]{2,1,0:T(8,128)(2,1)}, u32[]{:S(2)}, u32[]{:S(2)}) async-start(bf16[128,96,128]{2,1,0:T(8,128)(2,1)} %bitcast.29), calls=%async_computation.1 | async-start | bytes 6291456 | tf_op jit(solution)/shard_map/all_to_all | solution.py:803
  114.9 2.8 copy-start
  122.2 1.0 copy-start.2
  175.5 6.2 %copy-start.1 = (bf16[128,4096]{1,0:T(8,128)(2,1)S(1)}, bf16[128,4096]{1,0:T(8,128)(2,1)}, u32[]{:S(2)}) copy-start(bf16[128,4096]{1,0:T(8,128)(2,1)} %get-tuple-element.19.norm_ref) | copy-start | bytes 3145732
  175.5 6.2 %copy-start.6 = (bf16[4096,128]{1,0:T(8,128)(2,1)S(1)}, bf16[4096,128]{1,0:T(8,128)(2,1)}, u32[]{:S(2)}) copy-start(bf16[4096,128]{1,0:T(8,128)(2,1)} %router_ref.1) | copy-start | bytes 3145732
  175.5 50.1 %copy-start.3 = (bf16[128,4096]{1,0:T(8,128)(2,1)S(1)}, bf16[128,4096]{1,0:T(8,128)(2,1)}, u32[]{:S(2)}) copy-start(bf16[128,4096]{1,0:T(8,128)(2,1)} %get-tuple-element.21.hid_ref) | copy-start | bytes 3145732
  175.5 50.1 %copy-start.4 = (f32[128,128]{1,0:T(8,128)S(1)}, f32[128,128]{1,0:T(8,128)}, u32[]{:S(2)}) copy-start(f32[128,128]{1,0:T(8,128)} %get-tuple-element.22.rms_ref) | copy-start | bytes 196612
  175.6 50.1 %copy-start.5 = (f32[4096]{0:T(1024)S(1)}, f32[4096]{0:T(1024)}, u32[]{:S(2)}) copy-start(f32[4096]{0:T(1024)} %param.16) | copy-start | bytes 49156
  175.6 50.1 %all-to-all-start.3 = ((bf16[128,104,128]{2,1,0:T(8,128)(2,1)}), bf16[128,104,128]{2,1,0:T(8,128)(2,1)}, u32[]{:S(2)}, u32[]{:S(2)}) async-start(bf16[128,104,128]{2,1,0:T(8,128)(2,1)} %expert.1), calls=%async_computation.3 | async-start | bytes 6815744 | tf_op jit(solution)/shard_map/all_to_all | solution.py:803
  245.1 20.6 %collective-permute-start.3 = (bf16[8,128,512]{2,1,0:T(8,128)(2,1)}, bf16[8,128,512]{2,1,0:T(8,128)(2,1)S(1)}, u32[]{:S(2)}, u32[]{:S(2)}) collective-permute-start(bf16[8,128,512]{2,1,0:T(8,128)(2,1)} %get-tuple-element.29), channel_id=1, source_target_pairs={{0,1},{1,0},{2,3},{3,2},{4,5},{5,4},{6,7},{7,6},{8,9},{9,8},{10,11... | collective-permute-start | bytes 3145736 | tf_op jit(solution)/shard_map/ppermute | solution.py:799
  245.2 39.6 %all-to-all-start.5 = ((bf16[128,32,128]{2,1,0:T(8,128)(2,1)}), bf16[128,32,128]{2,1,0:T(8,128)(2,1)S(1)}, u32[]{:S(2)}, u32[]{:S(2)}) async-start(bf16[128,32,128]{2,1,0:T(8,128)(2,1)} %bitcast.18), calls=%async_computation.5 | async-start | bytes 2097152 | tf_op jit(solution)/shard_map/all_to_all | solution.py:803
  265.6 1.0 copy-start.7
  284.8 18.9 %all-to-all-start.4 = ((bf16[8,128,512]{2,1,0:T(8,128)(2,1)}), bf16[8,128,512]{2,1,0:T(8,128)(2,1)S(1)}, u32[]{:S(2)}, u32[]{:S(2)}) async-start(bf16[8,128,512]{2,1,0:T(8,128)(2,1)} %pair_sum.1), calls=%async_computation.4 | async-start | bytes 2097152 | tf_op jit(solution)/shard_map/all_to_all | solution.py:803
